TPU v7x, 32 devices: a whole 2x2x4 slice. The times are simulated.
32 devices in a mesh: groups: 2 (over x), seq: 16 (over z, y, core).
Axes of the slice: x: 2, y: 2, z: 4, core: 2. Of those that a mesh axis runs over, the one named last changes fastest.
Arguments:
- tokens: bfloat16 [32768, 1024], P(('groups', 'seq')), parts along dimension 0, may hold values from -6 to 6
- doc_start: int32 [32768], P(('groups', 'seq')), parts along dimension 0, may hold values from 0 to 1
- level_index: int32 [32768], P(('groups', 'seq')), parts along dimension 0, may hold values from 0 to 63
- level_table: float32 [64, 18], replicated, may hold values from 0.0004 to 4.1, as said below
- conv_weight: float32 [4, 1024], replicated, may hold values from -3 to 3
- query_weight: bfloat16 [1024, 1024], replicated, may hold values from -0.1875 to 0.1875
- key_weight: bfloat16 [1024, 1024], replicated, may hold values from -0.1875 to 0.1875
- value_weight: bfloat16 [1024, 1024], replicated, may hold values from -0.1875 to 0.1875
- norm_gain: float32 [1024], replicated, may hold values from 0.5 to 1.5
Outputs:
- mixed: bfloat16 [32768, 1024], P(('groups', 'seq')), parts along dimension 0
There are 2 independent parts, one for each index of `groups`. A program takes and returns all parts, laid end to end along the dimension named above; an argument that names none is the same for every part. Nothing has to cross between parts.
Inputs may be any that keep to these rules, and one draw needn't show every extreme that they name: `level_table`: positive entries.
All inputs are finite; a program needn't handle non-finite values.
Results may differ from a plain program's by a relative error of at most 0.007.
Values may be sent and summed in bfloat16 or wider, within the bound.
No kernel may reach another device: no remote copies, remote signals or barrier semaphores. Data moves between devices by JAX's collectives and lax.ppermute only.
A program may use at most 128 MiB of HBM per device.

v0:
```python
import jax
import jax.numpy as jnp
from jax import lax
from jax.sharding import PartitionSpec as P

HEADS = 8
HEAD_DIM = 128


highest = lax.Precision.HIGHEST
epsilon = 1e-05


def from_behind(value, axis, by):
    size = lax.axis_size(axis)
    pairs = [(i, i + by) for i in range(size) if 0 <= i + by < size]
    return lax.ppermute(value, axis, pairs)


def swapped(block, axis, apart):
    count = lax.axis_size(axis)
    route = []
    for low in range(count):
        high = low | 1 << apart
        if high != low and high < count:
            route += [(low, high), (high, low)]
    return lax.ppermute(block, axis, route)


def bit_count(values, bit_width):
    counted = jnp.zeros_like(values)
    for bit_index in range(bit_width):
        counted = counted + (values >= 1 << bit_index).astype(jnp.int32)
    return counted


def shards(
    tokens,
    doc_start,
    level_index,
    level_table,
    conv_weight,
    query_weight,
    key_weight,
    value_weight,
    norm_gain,
):
    row_count = tokens.shape[0]
    tap_count = conv_weight.shape[0]
    local_bits = row_count.bit_length() - 1
    local_doc = jnp.cumsum(doc_start)
    last_doc = local_doc[row_count - 1]
    rim_keep = (local_doc[row_count - tap_count + 1 :] == last_doc).astype(tokens.dtype)
    rim_rows = tokens[row_count - tap_count + 1 :] * rim_keep[:, None]
    carried = from_behind(rim_rows, "seq", 1)
    extended = jnp.concatenate([carried, tokens], 0)
    ext_doc = jnp.concatenate([jnp.zeros((tap_count - 1,), jnp.int32), local_doc], 0)
    conv_sum = jnp.zeros(tokens.shape, jnp.float32)
    for tap_index in range(tap_count):
        low_row = tap_count - 1 - tap_index
        same_doc = (ext_doc[low_row : low_row + row_count] == local_doc).astype(jnp.float32)
        conv_sum = (
            conv_sum
            + conv_weight[tap_index][None, :]
            * extended[low_row : low_row + row_count]
            * same_doc[:, None]
        )
    conv_out = conv_sum.astype(jnp.bfloat16)
    queries = (
        jnp.dot(conv_out, query_weight, preferred_element_type=jnp.float32)
        .astype(jnp.bfloat16)
        .reshape(row_count, HEADS, HEAD_DIM)
    )
    key_rows = (
        jnp.dot(conv_out, key_weight, preferred_element_type=jnp.float32)
        .astype(jnp.bfloat16)
        .reshape(row_count, HEADS, HEAD_DIM)
    )
    values = (
        jnp.dot(conv_out, value_weight, preferred_element_type=jnp.float32)
        .astype(jnp.bfloat16)
        .reshape(row_count, HEADS, HEAD_DIM)
    )
    onehot = (
        level_index[:, None] == jnp.arange(level_table.shape[0], dtype=jnp.int32)[None, :]
    ).astype(jnp.float32)
    level_weight = jnp.dot(
        onehot, level_table, precision=highest, preferred_element_type=jnp.float32
    )
    tail_mask = (local_doc == last_doc).astype(jnp.bfloat16)
    key_tail = key_rows * tail_mask[:, None, None]
    own_state = jnp.einsum("nhd,nhe->hde", key_tail, values, preferred_element_type=jnp.float32)
    own_open = (last_doc == 0).astype(jnp.float32)
    my_index = lax.axis_index("seq")
    chain_steps = lax.axis_size("seq").bit_length() - 1
    agg_state = own_state
    agg_open = own_open
    before_open = jnp.float32(1.0)
    level_states = []
    for bit_index in range(chain_steps):
        if bit_index < chain_steps - 1:
            other_state, other_open = swapped((agg_state, agg_open), "seq", bit_index)
        else:
            other_state, other_open = from_behind((agg_state, agg_open), "seq", 1 << bit_index)
        is_right = my_index // (1 << bit_index) % 2 == 1
        level_states.append(jnp.where(is_right, before_open, 0.0) * other_state)
        if bit_index < chain_steps - 1:
            left_state = jnp.where(is_right, other_state, agg_state)
            right_state = jnp.where(is_right, agg_state, other_state)
            left_open = jnp.where(is_right, other_open, agg_open)
            right_open = jnp.where(is_right, agg_open, other_open)
            before_open = before_open * jnp.where(is_right, other_open, 1.0)
            agg_state = right_state + right_open * left_state
            agg_open = left_open * right_open
    block_rows = min(512, row_count)
    key_pos = jnp.arange(row_count, dtype=jnp.int32)
    results = []
    for first_row in range(0, row_count, block_rows):
        query_pos = jnp.arange(first_row, first_row + block_rows, dtype=jnp.int32)
        level_of = bit_count(jnp.bitwise_xor(query_pos[:, None], key_pos[None, :]), local_bits)
        same_doc = (local_doc[first_row : first_row + block_rows, None] == local_doc[None, :]) & (
            query_pos[:, None] >= key_pos[None, :]
        )
        weight_rows = level_weight[first_row : first_row + block_rows]
        weight = jnp.zeros((block_rows, row_count), jnp.float32)
        for level_id in range(local_bits + 1):
            weight = weight + jnp.where(
                level_of == level_id, weight_rows[:, level_id : level_id + 1], 0.0
            )
        weight = jnp.where(same_doc, weight, 0.0)
        scores = jnp.einsum(
            "thd,shd->hts",
            queries[first_row : first_row + block_rows],
            key_rows,
            preferred_element_type=jnp.float32,
        )
        weighted = (scores * weight[None]).astype(jnp.bfloat16)
        results.append(
            jnp.einsum("hts,shd->thd", weighted, values, preferred_element_type=jnp.float32)
        )
    near_sum = jnp.concatenate(results, 0)
    token_gate = (local_doc == 0).astype(jnp.float32)
    query_wide = queries.astype(jnp.float32)
    combined = near_sum
    for bit_index, level_state in enumerate(level_states):
        product = jnp.einsum("thd,hde->the", query_wide, level_state, precision=highest)
        scale_now = level_weight[:, local_bits + 1 + bit_index] * token_gate
        combined = combined + scale_now[:, None, None] * product
    inv_norm = lax.rsqrt(jnp.mean(combined * combined, axis=-1, keepdims=True) + epsilon)
    gain_heads = norm_gain.reshape(HEADS, HEAD_DIM)
    return (
        (combined * inv_norm * gain_heads[None])
        .reshape(row_count, HEADS * HEAD_DIM)
        .astype(jnp.bfloat16)
    )


def solution(mesh):
    in_specs = (
        P(("groups", "seq"), None),
        P(("groups", "seq")),
        P(("groups", "seq")),
        P(),
        P(),
        P(),
        P(),
        P(),
        P(),
    )
    out_specs = P(("groups", "seq"), None)
    return jax.shard_map(shards, mesh=mesh, in_specs=in_specs, out_specs=out_specs, check_vma=False)
```

profile of v0, /device:TPU:24, one launch (start us, length us, event | category | flops | bytes accessed | tf_op | source)
XLA Modules:
  0.0 119.0 jit_solution(13723291301358879340)
XLA Ops:
  0.0 0.0 copy-start
  0.0 1.1 reduce-window.9
  1.1 0.1 slice.171
  1.2 0.1 slice_reduce_fusion
  1.3 1.2 fusion.41
  2.6 0.1 broadcast_select_fusion.3
  2.6 0.6 slice.174
  3.9 1.0 collective-permute-start.2
  4.9 0.7 compare_convert_fusion.1
  5.6 0.8 slice_multiply_fusion
  6.4 2.4 %collective-permute-start = (bf16[3,1024]{1,0:T(4,128)(2,1)S(1)}, bf16[3,1024]{1,0:T(4,128)(2,1)S(1)}, u32[]{:S(2)}, u32[]{:S(2)}) collective-permute-start(bf16[3,1024]{1,0:T(4,128)(2,1)S(1)} %slice_multiply_fusion), channel_id=1, source_target_pairs={{0,1},{1,2},{2,3},{3,4},{4,5},{5,6},{6,7},{7,8},{8,9},{9,10},{10,1... | collective-permute-start | bytes 18440 | tf_op jit(solution)/shard_map/ppermute | solution.py:17
  8.9 0.1 fusion.52
  9.0 0.9 fusion.57
  9.9 5.6 %add_select_fusion.1 = f32[512,1024]{1,0:T(8,128)} fusion(f32[512]{0:T(512)S(1)} %bitcast.109, f32[512]{0:T(512)S(1)} %bitcast.110, f32[512]{0:T(512)S(1)} %bitcast.111, f32[512]{0:T(512)S(1)} %bitcast.112, f32[512]{0:T(512)S(1)} %bitcast.113, f32[512]{0:T(512)S(1)} %bitcast.114, f32[512]{0:T(512)S(1)} %bitcast.115, f32[512]{0:T(512)S(1)} %bitcast.117, ...), kind=kLoop, calls=%fused_computation.32 | loop fusion | flops 34603008 | bytes 2125824 | tf_op jit(solution)/shard_map/jit(_where)/select_n | solution.py:130
  15.5 5.7 %add_select_fusion = f32[512,1024]{1,0:T(8,128)} fusion(f32[512]{0:T(512)S(1)} %bitcast.97, f32[512]{0:T(512)S(1)} %bitcast.98, f32[512]{0:T(512)S(1)} %bitcast.99, f32[512]{0:T(512)S(1)} %bitcast.100, f32[512]{0:T(512)S(1)} %bitcast.101, f32[512]{0:T(512)S(1)} %bitcast.102, f32[512]{0:T(512)S(1)} %bitcast.103, f32[512]{0:T(512)S(1)} %bitcast.104, ...), kind=kLoop, calls=%fused_computation.18 | loop fusion | flops 34603008 | bytes 2127872 | tf_op jit(solution)/shard_map/jit(_where)/select_n | solution.py:130
  21.2 0.6 compare_convert_fusion
  23.2 2.9 %collective-permute-start.4 = (f32[]{:T(128)}, f32[]{:T(128)}, u32[]{:S(2)}, u32[]{:S(2)}) collective-permute-start(f32[]{:T(128)} %mul.269), channel_id=1, source_target_pairs={{0,2},{2,0},{1,3},{3,1},{4,6},{6,4},{5,7},{7,5},{8,10},{10,8},{9,1... | collective-permute-start | bytes 20 | tf_op jit(solution)/shard_map/ppermute | solution.py:27
  26.7 0.2 collective-permute-done.4
  28.8 1.8 %collective-permute-start.6 = (f32[]{:T(128)}, f32[]{:T(128)}, u32[]{:S(2)}, u32[]{:S(2)}) collective-permute-start(f32[]{:T(128)} %mul.279), channel_id=1, source_target_pairs={{0,4},{4,0},{1,5},{5,1},{2,6},{6,2},{3,7},{7,3},{8,12},{12,8},{9,1... | collective-permute-start | bytes 20 | tf_op jit(solution)/shard_map/ppermute | solution.py:27
  30.6 1.9 %collective-permute-done.6 = f32[]{:T(128)} collective-permute-done((f32[]{:T(128)}, f32[]{:T(128)}, u32[]{:S(2)}, u32[]{:S(2)}) %collective-permute-start.6) | collective-permute-done | bytes 36 | tf_op jit(solution)/shard_map/ppermute | solution.py:27
  33.8 0.0 collective-permute-done
  33.8 7.6 %add_convert_fusion = bf16[1024,1024]{1,0:T(8,128)(2,1)S(1)} fusion(bf16[1024,1024]{1,0:T(8,128)(2,1)} %param.9, bf16[3,1024]{1,0:T(4,128)(2,1)S(1)} %collective-permute-done, f32[1024]{0:T(1024)S(1)} %get-tuple-element.43, f32[1024]{0:T(1024)S(1)} %bitcast.91, f32[1024]{0:T(1024)S(1)} %get-tuple-element.44, f32[1024]{0:T(1024)S(1)} %bitcast.92, ...), kind=kLoop, calls=%fused_computation.8 | loop fusion | flops 25165824 | bytes 4229120 | tf_op jit(solution)/shard_map/convert_element_type | solution.py:68
  41.5 0.0 copy-done
  41.5 0.0 copy-start.8
  41.5 2.4 %convolution_convert_fusion = bf16[1024,1024]{0,1:T(8,128)(2,1)S(1)} fusion(bf16[1024,1024]{1,0:T(8,128)(2,1)S(1)} %add_convert_fusion, bf16[1024,1024]{1,0:T(8,128)(2,1)S(1)} %copy-done), kind=kOutput, calls=%fused_computation.48 | convolution fusion | flops 2148532224 | bytes 6291456 | tf_op jit(solution)/shard_map/dot_general | solution.py:75
  43.9 0.0 copy-done.8
  43.9 0.0 copy-start.10
  43.9 2.4 %convolution_convert_fusion.2 = bf16[1024,1024]{0,1:T(8,128)(2,1)S(1)} fusion(bf16[1024,1024]{1,0:T(8,128)(2,1)S(1)} %add_convert_fusion, bf16[1024,1024]{1,0:T(8,128)(2,1)S(1)} %copy-done.8), kind=kOutput, calls=%fused_computation.50 | convolution fusion | flops 2148532224 | bytes 6291456 | tf_op jit(solution)/shard_map/dot_general | solution.py:80
  46.3 0.0 copy-start.11
  46.3 0.0 copy-done.10
  46.3 0.0 copy-start.9
  46.3 0.7 fusion.7
  47.0 0.6 copy-done.11
  47.6 0.0 collective-permute-start.1
  47.6 1.0 copy-done.9
  48.6 2.4 %convolution_convert_fusion.1 = bf16[1024,1024]{0,1:T(8,128)(2,1)S(1)} fusion(bf16[1024,1024]{1,0:T(8,128)(2,1)S(1)} %add_convert_fusion, bf16[1024,1024]{1,0:T(8,128)(2,1)S(1)} %copy-done.9), kind=kOutput, calls=%fused_computation.49 | convolution fusion | flops 2148532224 | bytes 6291456 | tf_op jit(solution)/shard_map/dot_general | solution.py:70
  51.0 0.0 copy-start.1
  51.0 1.6 %fusion.53 = (bf16[512,1024]{0,1:T(8,128)(2,1)}, bf16[512,1024]{0,1:T(8,128)(2,1)}) fusion(bf16[1024,1024]{0,1:T(8,128)(2,1)S(1)} %convolution_convert_fusion.1), kind=kLoop, calls=%fused_computation.94 | loop fusion | bytes 4194304 | tf_op jit(solution)/shard_map/slice | solution.py:133
  52.7 0.4 copy-done.1
  53.0 0.0 collective-permute-done.1
  53.0 0.8 copy-done.5
  53.9 0.1 multiply_add_fusion.2
  53.9 1.6 %collective-permute-start.3 = (f32[8,128,128]{2,1,0:T(8,128)S(1)}, f32[8,128,128]{2,1,0:T(8,128)}, u32[]{:S(2)}, u32[]{:S(2)}) collective-permute-start(f32[8,128,128]{2,1,0:T(8,128)S(1)} %multiply_add_fusion.2), channel_id=1, source_target_pairs={{0,2},{2,0},{1,3},{3,1},{4,6},{6,4},{5,7},{7,5},{8,10},{10,8},{9,1... | collective-permute-start | bytes 1572872 | tf_op jit(solution)/shard_map/ppermute | solution.py:27
  55.5 9.6 %fusion.32 = f32[512,8,128]{0,2,1:T(8,128)} fusion(bf16[1024,8,128]{0,2,1:T(8,128)(2,1)} %bitcast.125, bf16[512,8,128]{0,2,1:T(8,128)(2,1)} %bitcast.83, bf16[1024,8,128]{0,2,1:T(8,128)(2,1)} %bitcast.122, f32[512,1024]{1,0:T(8,128)} %add_select_fusion.1), kind=kOutput, calls=%fused_computation.52 | convolution fusion | flops 2155872256 | bytes 9437184 | tf_op jit(solution)/shard_map/hts,shd->thd/dot_general | solution.py:139
  65.1 2.3 %collective-permute-done.3 = f32[8,128,128]{2,1,0:T(8,128)} collective-permute-done((f32[8,128,128]{2,1,0:T(8,128)S(1)}, f32[8,128,128]{2,1,0:T(8,128)}, u32[]{:S(2)}, u32[]{:S(2)}) %collective-permute-start.3) | collective-permute-done | bytes 524320 | tf_op jit(solution)/shard_map/ppermute | solution.py:27
  67.4 1.1 multiply_add_fusion.1
  68.6 0.5 collective-permute-start.5
  69.1 9.6 %fusion.31 = f32[512,8,128]{0,2,1:T(8,128)} fusion(bf16[1024,8,128]{0,2,1:T(8,128)(2,1)} %bitcast.126, bf16[512,8,128]{0,2,1:T(8,128)(2,1)} %bitcast.82, bf16[1024,8,128]{0,2,1:T(8,128)(2,1)} %bitcast.123, f32[512,1024]{1,0:T(8,128)} %add_select_fusion), kind=kOutput, calls=%fused_computation.51 | convolution fusion | flops 2155872256 | bytes 9437184 | tf_op jit(solution)/shard_map/hts,shd->thd/dot_general | solution.py:139
  78.6 0.0 copy-done.6
  78.6 3.6 %fusion.39 = f32[8,128,1024]{2,1,0:T(8,128)S(1)} fusion(bf16[1024,8,128]{0,2,1:T(8,128)(2,1)} %bitcast.77, f32[8,128,128]{2,1,0:T(8,128)S(1)} %copy-done.6, f32[]{:T(128)S(6)} %select_n.295), kind=kOutput, calls=%fused_computation.62 | convolution fusion | flops 1610743808 | bytes 6815748 | tf_op jit(solution)/shard_map/thd,hde->the/dot_general | solution.py:146
  82.3 0.0 collective-permute-done.5
  82.3 1.1 multiply_add_fusion
  83.4 1.6 %collective-permute-start.7 = (f32[8,128,128]{2,1,0:T(8,128)S(1)}, f32[8,128,128]{2,1,0:T(8,128)S(1)}, u32[]{:S(2)}, u32[]{:S(2)}) collective-permute-start(f32[8,128,128]{2,1,0:T(8,128)S(1)} %multiply_add_fusion), channel_id=1, source_target_pairs={{0,8},{1,9},{2,10},{3,11},{4,12},{5,13},{6,14},{7,15},{16,24},{17,... | collective-permute-start | bytes 1572872 | tf_op jit(solution)/shard_map/ppermute | solution.py:17
  85.0 0.0 copy-done.2
  85.0 3.0 %fusion.37 = f32[8,128,1024]{2,1,0:T(8,128)S(1)} fusion(bf16[1024,8,128]{0,2,1:T(8,128)(2,1)S(1)} %bitcast.78, f32[8,128,128]{2,1,0:T(8,128)} %collective-permute-done.3, f32[]{:T(128)S(6)} %select_n.299), kind=kOutput, calls=%fused_computation.59 | convolution fusion | flops 1610743808 | bytes 6815748 | tf_op jit(solution)/shard_map/thd,hde->the/dot_general | solution.py:146
  88.0 0.0 copy-start.3
  88.0 0.0 copy-start.4
  88.0 3.1 %fusion.35 = f32[8,128,1024]{2,1,0:T(8,128)S(1)} fusion(bf16[1024,8,128]{0,2,1:T(8,128)(2,1)S(1)} %bitcast.79, f32[8,128,128]{2,1,0:T(8,128)} %collective-permute-done.5, f32[]{:T(128)S(6)} %select_n.308), kind=kOutput, calls=%fused_computation.56 | convolution fusion | flops 1610743808 | bytes 6815748 | tf_op jit(solution)/shard_map/thd,hde->the/dot_general | solution.py:146
  91.1 18.6 %collective-permute-done.7 = f32[8,128,128]{2,1,0:T(8,128)S(1)} collective-permute-done((f32[8,128,128]{2,1,0:T(8,128)S(1)}, f32[8,128,128]{2,1,0:T(8,128)S(1)}, u32[]{:S(2)}, u32[]{:S(2)}) %collective-permute-start.7) | collective-permute-done | bytes 524320 | tf_op jit(solution)/shard_map/ppermute | solution.py:17
  109.6 0.0 copy-done.3
  109.6 0.0 copy-done.4
  109.7 3.5 %multiply_reduce_fusion = (f32[1024,8]{0,1:T(8,128)S(1)}, f32[1024,8,128]{0,2,1:T(8,128)S(1)}) fusion(bf16[1024,8,128]{0,2,1:T(8,128)(2,1)S(1)} %bitcast.80, f32[8,128,128]{2,1,0:T(8,128)S(1)} %collective-permute-done.7, f32[]{:T(128)S(6)} %select_n.317, f32[1024]{0:T(1024)S(1)} %get-tuple-element.47, f32[8,128,1024]{2,1,0:T(8,128)S(1)} %fusion.35, ...), kind=kOutput, calls=%fused_computation.7 | convolution fusion | flops 1622269952 | bytes 23642116 | tf_op jit(solution)/shard_map/thd,hde->the/dot_general | solution.py:146
  113.2 1.9 %multiply_convert_fusion.2 = bf16[1024,8,128]{0,2,1:T(8,128)(2,1)} fusion(f32[1024,8,128]{0,2,1:T(8,128)S(1)} %get-tuple-element.49, f32[8,128]{1,0:T(8,128)S(1)} %bitcast.120, f32[1024,8]{0,1:T(8,128)S(1)} %add_rsqrt_fusion), kind=kLoop, calls=%fused_computation.6 | loop fusion | flops 3145728 | bytes 6328320 | tf_op jit(solution)/shard_map/convert_element_type | solution.py:154
  115.1 3.9 %copy.29 = bf16[1024,1024]{1,0:T(8,128)(2,1)} copy(bf16[1024,1024]{0,1:T(8,128)(2,1)} %bitcast.81) | data formatting | bytes 4194304 | tf_op jit(solution)/shard_map/convert_element_type | solution.py:154
  (14 shorter events, 0.1 us)
Async XLA Ops:
  0.0 41.5 %copy-start = (bf16[1024,1024]{1,0:T(8,128)(2,1)S(1)}, bf16[1024,1024]{1,0:T(8,128)(2,1)}, u32[]{:S(2)}) copy-start(bf16[1024,1024]{1,0:T(8,128)(2,1)} %param.15) | copy-start | bytes 6291460
  3.9 18.0 %collective-permute-start.2 = (f32[]{:T(128)}, f32[]{:T(128)}, u32[]{:S(2)}, u32[]{:S(2)}) collective-permute-start(f32[]{:T(128)} %convert_element_type.636), channel_id=1, source_target_pairs={{0,1},{1,0},{2,3},{3,2},{4,5},{5,4},{6,7},{7,6},{8,9},{9,8},{10,11... | collective-permute-start | bytes 20 | tf_op jit(solution)/shard_map/ppermute | solution.py:27
  6.4 27.4 %collective-permute-start = (bf16[3,1024]{1,0:T(4,128)(2,1)S(1)}, bf16[3,1024]{1,0:T(4,128)(2,1)S(1)}, u32[]{:S(2)}, u32[]{:S(2)}) collective-permute-start(bf16[3,1024]{1,0:T(4,128)(2,1)S(1)} %slice_multiply_fusion), channel_id=1, source_target_pairs={{0,1},{1,2},{2,3},{3,4},{4,5},{5,6},{6,7},{7,8},{8,9},{9,10},{10,1... | collective-permute-start | bytes 18440 | tf_op jit(solution)/shard_map/ppermute | solution.py:17
  23.2 3.7 %collective-permute-start.4 = (f32[]{:T(128)}, f32[]{:T(128)}, u32[]{:S(2)}, u32[]{:S(2)}) collective-permute-start(f32[]{:T(128)} %mul.269), channel_id=1, source_target_pairs={{0,2},{2,0},{1,3},{3,1},{4,6},{6,4},{5,7},{7,5},{8,10},{10,8},{9,1... | collective-permute-start | bytes 20 | tf_op jit(solution)/shard_map/ppermute | solution.py:27
  28.8 3.7 %collective-permute-start.6 = (f32[]{:T(128)}, f32[]{:T(128)}, u32[]{:S(2)}, u32[]{:S(2)}) collective-permute-start(f32[]{:T(128)} %mul.279), channel_id=1, source_target_pairs={{0,4},{4,0},{1,5},{5,1},{2,6},{6,2},{3,7},{7,3},{8,12},{12,8},{9,1... | collective-permute-start | bytes 20 | tf_op jit(solution)/shard_map/ppermute | solution.py:27
  41.5 2.4 %copy-start.8 = (bf16[1024,1024]{1,0:T(8,128)(2,1)S(1)}, bf16[1024,1024]{1,0:T(8,128)(2,1)}, u32[]{:S(2)}) copy-start(bf16[1024,1024]{1,0:T(8,128)(2,1)} %param.16) | copy-start | bytes 6291460
  43.9 2.4 %copy-start.10 = (bf16[1024,1024]{0,1:T(8,128)(2,1)}, bf16[1024,1024]{0,1:T(8,128)(2,1)S(1)}, u32[]{:S(2)}) copy-start(bf16[1024,1024]{0,1:T(8,128)(2,1)S(1)} %convolution_convert_fusion) | copy-start | bytes 6291460
  46.3 1.4 %copy-start.11 = (bf16[1024,1024]{0,1:T(8,128)(2,1)}, bf16[1024,1024]{0,1:T(8,128)(2,1)S(1)}, u32[]{:S(2)}) copy-start(bf16[1024,1024]{0,1:T(8,128)(2,1)S(1)} %convolution_convert_fusion.2) | copy-start | bytes 6291460
  46.3 2.3 %copy-start.9 = (bf16[1024,1024]{1,0:T(8,128)(2,1)S(1)}, bf16[1024,1024]{1,0:T(8,128)(2,1)}, u32[]{:S(2)}) copy-start(bf16[1024,1024]{1,0:T(8,128)(2,1)} %param.14) | copy-start | bytes 6291460
  47.6 5.4 %collective-permute-start.1 = (f32[8,128,128]{2,1,0:T(8,128)S(1)}, f32[8,128,128]{2,1,0:T(8,128)S(1)}, u32[]{:S(2)}, u32[]{:S(2)}) collective-permute-start(f32[8,128,128]{2,1,0:T(8,128)S(1)} %fusion.7), channel_id=1, source_target_pairs={{0,1},{1,0},{2,3},{3,2},{4,5},{5,4},{6,7},{7,6},{8,9},{9,8},{10,11... | collective-permute-start | bytes 1572872 | tf_op jit(solution)/shard_map/ppermute | solution.py:27
  51.0 2.0 %copy-start.1 = (bf16[1024,1024]{0,1:T(8,128)(2,1)}, bf16[1024,1024]{0,1:T(8,128)(2,1)S(1)}, u32[]{:S(2)}) copy-start(bf16[1024,1024]{0,1:T(8,128)(2,1)S(1)} %convolution_convert_fusion.1) | copy-start | bytes 6291460
  53.0 0.8 copy-start.5
  53.9 13.5 %collective-permute-start.3 = (f32[8,128,128]{2,1,0:T(8,128)S(1)}, f32[8,128,128]{2,1,0:T(8,128)}, u32[]{:S(2)}, u32[]{:S(2)}) collective-permute-start(f32[8,128,128]{2,1,0:T(8,128)S(1)} %multiply_add_fusion.2), channel_id=1, source_target_pairs={{0,2},{2,0},{1,3},{3,1},{4,6},{6,4},{5,7},{7,5},{8,10},{10,8},{9,1... | collective-permute-start | bytes 1572872 | tf_op jit(solution)/shard_map/ppermute | solution.py:27
  68.6 13.7 %collective-permute-start.5 = (f32[8,128,128]{2,1,0:T(8,128)S(1)}, f32[8,128,128]{2,1,0:T(8,128)}, u32[]{:S(2)}, u32[]{:S(2)}) collective-permute-start(f32[8,128,128]{2,1,0:T(8,128)S(1)} %multiply_add_fusion.1), channel_id=1, source_target_pairs={{0,4},{4,0},{1,5},{5,1},{2,6},{6,2},{3,7},{7,3},{8,12},{12,8},{9,1... | collective-permute-start | bytes 1572872 | tf_op jit(solution)/shard_map/ppermute | solution.py:27
  69.1 9.6 %copy-start.6 = (f32[8,128,128]{2,1,0:T(8,128)S(1)}, f32[8,128,128]{2,1,0:T(8,128)}, u32[]{:S(2)}) copy-start(f32[8,128,128]{2,1,0:T(8,128)} %copy-done.5) | copy-start | bytes 1572868
  78.6 6.3 %copy-start.2 = (bf16[1024,1024]{0,1:T(8,128)(2,1)S(1)}, bf16[1024,1024]{0,1:T(8,128)(2,1)}, u32[]{:S(2)}) copy-start(bf16[1024,1024]{0,1:T(8,128)(2,1)} %copy-done.1) | copy-start | bytes 6291460
  83.4 26.2 %collective-permute-start.7 = (f32[8,128,128]{2,1,0:T(8,128)S(1)}, f32[8,128,128]{2,1,0:T(8,128)S(1)}, u32[]{:S(2)}, u32[]{:S(2)}) collective-permute-start(f32[8,128,128]{2,1,0:T(8,128)S(1)} %multiply_add_fusion), channel_id=1, source_target_pairs={{0,8},{1,9},{2,10},{3,11},{4,12},{5,13},{6,14},{7,15},{16,24},{17,... | collective-permute-start | bytes 1572872 | tf_op jit(solution)/shard_map/ppermute | solution.py:17
  88.0 21.7 %copy-start.3 = (f32[512,8,128]{0,2,1:T(8,128)S(1)}, f32[512,8,128]{0,2,1:T(8,128)}, u32[]{:S(2)}) copy-start(f32[512,8,128]{0,2,1:T(8,128)} %fusion.32) | copy-start | bytes 6291460
  88.0 21.7 %copy-start.4 = (f32[512,8,128]{0,2,1:T(8,128)S(1)}, f32[512,8,128]{0,2,1:T(8,128)}, u32[]{:S(2)}) copy-start(f32[512,8,128]{0,2,1:T(8,128)} %fusion.31) | copy-start | bytes 6291460
  109.7 3.5 %copy-start.7 = (f32[1024]{0:T(1024)S(1)}, f32[1024]{0:T(1024)}, u32[]{:S(2)}) copy-start(f32[1024]{0:T(1024)} %param.17) | copy-start | bytes 12292
where the time goes:
time: 120 us; the launch traced here: 119 us
  matrix products  41.4 us (34%)
  other arithmetic  26.6 us (22%)
  waiting for transfers between devices  23 us (19%)
  starting transfers between devices  11.8 us (10%)
  local copies, waits for them, and re-layouts  10.1 us (8%)
  between operations  6.1 us (5%)
    dot_general x2, matrix products, shards(): jnp.einsum('hts,shd->thd', weighted, values, preferred_element_type=jnp.f...  19.1 us
    ppermute x2, waiting for transfers between devices, from_behind(): return lax.ppermute(value, axis, pairs)  18.6 us
    dot_general x4, matrix products, shards(): jnp.einsum('thd,hde->the', query_wide, level_state, precision=highest)  13.2 us
    select_n x2, other arithmetic, shards(): weight = jnp.where(same_doc, weight, 0.0)  11.3 us
    ppermute x6, starting transfers between devices, swapped(): return lax.ppermute(block, axis, route)  7.83 us
    convert_element_type x1, other arithmetic, shards(): conv_out = conv_sum.astype(jnp.bfloat16)  7.63 us
    ppermute x6, waiting for transfers between devices, swapped(): return lax.ppermute(block, axis, route)  4.49 us
    ppermute x2, starting transfers between devices, from_behind(): return lax.ppermute(value, axis, pairs)  3.95 us
  transfers between devices with their start and end apart: 8, of which 4 were waited for; matrix products, arithmetic and copies ran while one was open for 40% of the time, Pallas kernels for 0%

commit v1 on v0

v1 whole, which is shorter than its diff:
```python
import functools

import jax
import jax.numpy as jnp
from jax import lax
from jax.experimental import pallas as pl
from jax.experimental.pallas import tpu as pltpu
from jax.sharding import PartitionSpec as P

HEADS = 8
HEAD_DIM = 128
CHUNK = 256
FLAG_ROWS = 16
DOC_COL = 32
highest = lax.Precision.HIGHEST
epsilon = 1e-05
F32 = jnp.float32
BF16 = jnp.bfloat16


def dot(a, b, dims=((1,), (0,)), precision=None):
    return lax.dot_general(a, b, (dims, ((), ())), precision=precision, preferred_element_type=F32)


def state_kernel(
    x_ref, halo_ref, ds_ref, idx_ref, table_ref, cw_ref, wk_hbm, wv_hbm,
    conv_ref, k_ref, v_ref, aux_ref, pay_ref, loc_ref,
    wk_ref, wv_ref, xs, feat, coef, st, sems,
):
    rows, width = x_ref.shape
    chunks = rows // CHUNK
    taps = cw_ref.shape[0]
    table_rows, levels = table_ref.shape
    half = HEADS // 2 * HEAD_DIM
    copy_k = pltpu.make_async_copy(wk_hbm, wk_ref, sems.at[0])
    copy_v = pltpu.make_async_copy(wv_hbm, wv_ref, sems.at[1])
    copy_k.start()
    copy_v.start()

    xs[0:8, :] = halo_ref[...].astype(F32)
    for c in range(chunks):
        xs[8 + c * CHUNK : 8 + (c + 1) * CHUNK, :] = x_ref[c * CHUNK : (c + 1) * CHUNK, :].astype(F32)

    starts = ds_ref[...].astype(F32)
    upper = (
        lax.broadcasted_iota(jnp.int32, (CHUNK, CHUNK), 0)
        <= lax.broadcasted_iota(jnp.int32, (CHUNK, CHUNK), 1)
    ).astype(BF16)
    starts8 = jnp.broadcast_to(starts, (8, rows))
    lane = lax.broadcasted_iota(jnp.int32, (8, rows), 1)
    base = jnp.zeros((8, 1), F32)
    docs = []
    for c in range(chunks):
        part = dot(starts8[:, c * CHUNK : (c + 1) * CHUNK].astype(BF16), upper) + base
        docs.append(part)
        base = part[:, CHUNK - 1 : CHUNK]
    doc8 = jnp.concatenate(docs, axis=1)
    same = [1.0 - starts8]
    for back in range(1, taps - 1):
        moved = pltpu.roll(same[0], back, axis=1)
        same.append(same[-1] * jnp.where(lane < back, 1.0, moved))
    sub = lax.broadcasted_iota(jnp.int32, (8, rows), 0)
    extra = jnp.where(sub == 0, doc8, 0.0)
    for n, m in enumerate(same):
        extra = jnp.where(sub == n + 1, m, extra)
    idx = jnp.broadcast_to(idx_ref[...], (table_rows, rows))
    feat[0:table_rows, :] = (idx == lax.broadcasted_iota(jnp.int32, (table_rows, rows), 0)).astype(F32)
    feat[table_rows : table_rows + 8, :] = extra
    coef[...] = jnp.zeros_like(coef)
    coef[0:table_rows, 0:levels] = table_ref[...]
    coef[table_rows : table_rows + 8, :] = (
        lax.broadcasted_iota(jnp.int32, (8, 128), 0) + DOC_COL
        == lax.broadcasted_iota(jnp.int32, (8, 128), 1)
    ).astype(F32)
    for c in range(chunks):
        aux_ref[c * CHUNK : (c + 1) * CHUNK, :] = dot(
            feat[:, c * CHUNK : (c + 1) * CHUNK], coef[...], ((0,), (0,)), highest
        )

    ends = []
    for c in range(chunks):
        low = c * CHUNK
        masks = [
            jnp.broadcast_to(aux_ref[low : low + CHUNK, DOC_COL + n : DOC_COL + n + 1], (CHUNK, 128))
            for n in range(1, taps)
        ]
        for j in range(0, width, 128):
            total = xs[8 + low : 8 + low + CHUNK, j : j + 128] * cw_ref[0:1, j : j + 128]
            for n in range(1, taps):
                total = total + (
                    xs[8 + low - n : 8 + low - n + CHUNK, j : j + 128] * cw_ref[n : n + 1, j : j + 128]
                ) * masks[n - 1]
            conv_ref[low : low + CHUNK, j : j + 128] = total.astype(BF16)
        ends.append(aux_ref[low + CHUNK - 1 : low + CHUNK, DOC_COL : DOC_COL + 1])
    copy_k.wait()
    copy_v.wait()
    for c in range(chunks):
        low = c * CHUNK
        tail = (aux_ref[low : low + CHUNK, DOC_COL : DOC_COL + 1] == ends[c]).astype(F32)
        tail = jnp.broadcast_to(tail, (CHUNK, 2 * HEAD_DIM))
        conv = conv_ref[low : low + CHUNK, :]
        for h in range(0, HEADS, 2):
            cols = slice(h * HEAD_DIM, (h + 2) * HEAD_DIM)
            key = dot(conv, wk_ref[:, cols])
            value = dot(conv, wv_ref[:, cols]).astype(BF16)
            k_ref[low : low + CHUNK, cols] = key.astype(BF16)
            v_ref[low : low + CHUNK, cols] = value
            kept = (key * tail).astype(BF16)
            for g in range(2):
                lanes = slice(g * HEAD_DIM, (g + 1) * HEAD_DIM)
                st[c, (h + g) * HEAD_DIM : (h + g + 1) * HEAD_DIM, :] = dot(
                    kept[:, lanes], value[:, lanes], ((0,), (0,))
                )

    nodes = [(st[c], ends[c], c) for c in range(chunks)]
    slot = 0
    while len(nodes) > 1:
        merged = []
        for n in range(0, len(nodes), 2):
            left, left_end, _ = nodes[n]
            right, right_end, last = nodes[n + 1]
            loc_ref[slot] = left.astype(BF16)
            slot += 1
            keep = (left_end == right_end).astype(F32)
            merged.append((right + keep * left, right_end, last))
        nodes = merged
    total = nodes[0][0].astype(BF16)
    closed = jnp.broadcast_to((ends[-1] > 0).astype(F32), (FLAG_ROWS, HEAD_DIM)).astype(BF16)
    for n in range(2):
        pay_ref[n, 0:half, :] = total[n * half : (n + 1) * half]
        pay_ref[n, half : half + FLAG_ROWS, :] = closed


def near_kernel(conv_ref, wq_ref, k_ref, v_ref, aux_ref, loc_ref, doc_ref, q_ref, near_ref, weight):
    rows = conv_ref.shape[0]
    chunks = rows // CHUNK
    bits = CHUNK.bit_length() - 1

    @pl.when(pl.program_id(0) == 0)
    def _():
        t = lax.broadcasted_iota(jnp.int32, (CHUNK, CHUNK), 0)
        s = lax.broadcasted_iota(jnp.int32, (CHUNK, CHUNK), 1)
        gap = jnp.bitwise_xor(t, s)
        for c in range(chunks):
            low = c * CHUNK
            lam = aux_ref[low : low + CHUNK, :]
            w = jnp.broadcast_to(lam[:, 0:1], (CHUNK, CHUNK))
            for level in range(1, bits + 1):
                w = jnp.where(gap >= 1 << (level - 1), lam[:, level : level + 1], w)
            same = (lam[:, DOC_COL : DOC_COL + 1] == doc_ref[0:1, low : low + CHUNK]) & (t >= s)
            weight[c] = jnp.where(same, w, 0.0)

    query = dot(conv_ref[...], wq_ref[...]).astype(BF16)
    q_ref[...] = query
    for c in range(chunks):
        low = c * CHUNK
        lam = aux_ref[low : low + CHUNK, :]
        doc = lam[:, DOC_COL : DOC_COL + 1]
        gates = []
        slot, count, level = 0, chunks, bits + 1
        while count > 1:
            node = c * count // chunks
            if node % 2 == 1:
                last = node * (chunks // count) * CHUNK - 1
                end = aux_ref[last : last + 1, DOC_COL : DOC_COL + 1]
                gate = jnp.where(doc == end, lam[:, level : level + 1], 0.0)
                gates.append((slot + node // 2, jnp.broadcast_to(gate, (CHUNK, HEAD_DIM))))
            slot += count // 2
            count //= 2
            level += 1
        for g in range(2):
            lanes = slice(g * HEAD_DIM, (g + 1) * HEAD_DIM)
            q = query[low : low + CHUNK, lanes]
            scores = dot(q, k_ref[low : low + CHUNK, lanes], ((1,), (1,)))
            weighted = (scores * weight[c]).astype(BF16)
            total = dot(weighted, v_ref[low : low + CHUNK, lanes])
            for n, gate in gates:
                total = total + gate * dot(q, loc_ref[n, g * HEAD_DIM : (g + 1) * HEAD_DIM, :])
            near_ref[low : low + CHUNK, lanes] = total


def far_kernel(first_level, q_ref, near_ref, aux_ref, gain_ref, *refs):
    states, out_ref = refs[:-1], refs[-1]
    rows = q_ref.shape[0]
    for low in range(0, rows, CHUNK):
        lam = aux_ref[low : low + CHUNK, :]
        gate = (lam[:, DOC_COL : DOC_COL + 1] == 0.0).astype(F32)
        scales = [
            jnp.broadcast_to(lam[:, first_level + n : first_level + n + 1] * gate, (CHUNK, HEAD_DIM))
            for n in range(len(states))
        ]
        for g in range(2):
            lanes = slice(g * HEAD_DIM, (g + 1) * HEAD_DIM)
            q = q_ref[low : low + CHUNK, lanes]
            total = near_ref[low : low + CHUNK, lanes]
            for scale, state in zip(scales, states):
                total = total + scale * dot(q, state[0, g * HEAD_DIM : (g + 1) * HEAD_DIM, :])
            mean = jnp.mean(total * total, axis=-1, keepdims=True)
            total = total * lax.rsqrt(mean + epsilon) * gain_ref[0:1, lanes]
            out_ref[low : low + CHUNK, lanes] = total.astype(BF16)


def crossed(block, mask):
    size = lax.axis_size("seq")
    return lax.ppermute(block, "seq", [(i, i ^ mask) for i in range(size)])


def joined(own, other, is_right):
    right = jnp.where(is_right, own, other).astype(F32)
    left = jnp.where(is_right, other, own).astype(F32)
    index = (0,) * (own.ndim - 2)
    keep = 1.0 - right[index + (right.shape[-2] - 1, 0)]
    return (right + keep * left).astype(BF16)


def flag_of(block):
    return block[(0,) * (block.ndim - 2) + (block.shape[-2] - 1, 0)].astype(F32)


def shards(
    tokens,
    doc_start,
    level_index,
    level_table,
    conv_weight,
    query_weight,
    key_weight,
    value_weight,
    norm_gain,
):
    rows, width = tokens.shape
    taps = conv_weight.shape[0]
    chunks = rows // CHUNK
    local_bits = rows.bit_length() - 1
    half = HEADS // 2 * HEAD_DIM
    size = lax.axis_size("seq")
    me = lax.axis_index("seq")
    steps = size.bit_length() - 1
    VMEM = pl.BlockSpec(memory_space=pltpu.VMEM)
    ANY = pl.BlockSpec(memory_space=pl.ANY)

    tail = doc_start[rows - 8 :]
    later = jnp.arange(8)[:, None] < jnp.arange(8)[None, :]
    keep = (jnp.sum(jnp.where(later, tail[None, :], 0), axis=1) == 0).astype(tokens.dtype)
    rim = tokens[rows - 8 :] * keep[:, None]
    halo = lax.ppermute(rim, "seq", [(i, i + 1) for i in range(size - 1)])

    starts = doc_start.reshape(1, rows)
    conv, key_rows, values, aux, payload, local_states = pl.pallas_call(
        state_kernel,
        out_shape=(
            jax.ShapeDtypeStruct((rows, width), BF16),
            jax.ShapeDtypeStruct((rows, width), BF16),
            jax.ShapeDtypeStruct((rows, width), BF16),
            jax.ShapeDtypeStruct((rows, 128), F32),
            jax.ShapeDtypeStruct((2, half + FLAG_ROWS, HEAD_DIM), BF16),
            jax.ShapeDtypeStruct((chunks - 1, HEADS * HEAD_DIM, HEAD_DIM), BF16),
        ),
        in_specs=[VMEM] * 6 + [ANY] * 2,
        out_specs=(VMEM,) * 6,
        scratch_shapes=[
            pltpu.VMEM((width, width), BF16),
            pltpu.VMEM((width, width), BF16),
            pltpu.VMEM((rows + 8, width), F32),
            pltpu.VMEM((level_table.shape[0] + 8, rows), F32),
            pltpu.VMEM((level_table.shape[0] + 8, 128), F32),
            pltpu.VMEM((chunks, HEADS * HEAD_DIM, HEAD_DIM), F32),
            pltpu.SemaphoreType.DMA((2,)),
        ],
        compiler_params=pltpu.CompilerParams(vmem_limit_bytes=48 << 20),
        cost_estimate=pl.CostEstimate(
            flops=4 * rows * width * width, bytes_accessed=8 * width * width, transcendentals=0
        ),
        name="conv_key_value_state",
    )(
        tokens,
        halo,
        starts,
        level_index.reshape(1, rows),
        level_table,
        conv_weight,
        key_weight,
        value_weight,
    )

    core = me % 2
    other = crossed(payload, 1)
    is_right = core == 1
    before = jnp.float32(1.0)
    level_states = [(other.astype(F32) * jnp.where(is_right, 1.0, 0.0)).astype(BF16)]
    both = joined(payload, other, is_right)
    before = before * jnp.where(is_right, 1.0 - flag_of(other), 1.0)
    agg = jnp.where(is_right, both[1], both[0])
    for bit in range(1, steps):
        last = bit == steps - 1
        mask = 1 << bit
        if last and bit >= 2:
            mask |= 1 << (bit - 1)
        other = crossed(agg, mask)
        is_right = (me >> bit) % 2 == 1
        mate = crossed(other, 1)
        gate = before * jnp.where(is_right, 1.0, 0.0)
        pair = jnp.where(core == 1, jnp.stack([mate, other]), jnp.stack([other, mate]))
        level_states.append((pair.astype(F32) * gate).astype(BF16))
        before = before * jnp.where(is_right, 1.0 - flag_of(other), 1.0)
        if not last:
            agg = joined(agg, other, is_right)

    docs = jnp.cumsum(doc_start).astype(F32).reshape(1, rows)
    pairs = HEADS // 2
    wide = 2 * HEAD_DIM
    column = pl.BlockSpec((rows, wide), lambda i: (0, i))
    query, near = pl.pallas_call(
        near_kernel,
        grid=(pairs,),
        out_shape=(
            jax.ShapeDtypeStruct((rows, width), BF16),
            jax.ShapeDtypeStruct((rows, width), F32),
        ),
        in_specs=[
            pl.BlockSpec((rows, width), lambda i: (0, 0)),
            column,
            column,
            column,
            pl.BlockSpec((rows, 128), lambda i: (0, 0)),
            pl.BlockSpec((chunks - 1, wide, HEAD_DIM), lambda i: (0, i, 0)),
            pl.BlockSpec((1, rows), lambda i: (0, 0)),
        ],
        out_specs=(column, column),
        scratch_shapes=[pltpu.VMEM((chunks, CHUNK, CHUNK), F32)],
        compiler_params=pltpu.CompilerParams(vmem_limit_bytes=40 << 20),
        cost_estimate=pl.CostEstimate(
            flops=4 * rows * width * width, bytes_accessed=8 * width * width, transcendentals=0
        ),
        name="query_near",
    )(conv, query_weight, key_rows, values, aux, local_states, docs)

    state_spec = pl.BlockSpec((1, wide, HEAD_DIM), lambda i: (i // 2, i % 2, 0))
    return pl.pallas_call(
        functools.partial(far_kernel, local_bits + 1),
        grid=(pairs,),
        out_shape=jax.ShapeDtypeStruct((rows, width), BF16),
        in_specs=[
            column,
            column,
            pl.BlockSpec((rows, 128), lambda i: (0, 0)),
            pl.BlockSpec((1, wide), lambda i: (0, i)),
        ]
        + [state_spec] * steps,
        out_specs=column,
        compiler_params=pltpu.CompilerParams(vmem_limit_bytes=40 << 20),
        cost_estimate=pl.CostEstimate(
            flops=2 * rows * width * width, bytes_accessed=8 * width * width, transcendentals=0
        ),
        name="far_norm",
    )(query, near, aux, norm_gain.reshape(1, width), *level_states)


def solution(mesh):
    split = P(("groups", "seq"))
    in_specs = (P(("groups", "seq"), None), split, split, P(), P(), P(), P(), P(), P())
    return jax.shard_map(
        shards, mesh=mesh, in_specs=in_specs, out_specs=P(("groups", "seq"), None), check_vma=False
    )
```

time: 120 us -> 92.2 us (0.77)
  the two profiles are of different devices: /device:TPU:24 before, /device:TPU:0 now
where the time goes in v1:
time: 92.2 us; the launch traced here: 91.5 us
  Pallas kernels  38.6 us (42%)
  local copies, waits for them, and re-layouts  20.8 us (23%)
  starting transfers between devices  15 us (16%)
  waiting for transfers between devices  7.53 us (8%)
  other arithmetic  5.72 us (6%)
  between operations  3.84 us (4%)
    unnamed x31, local copies, waits for them, and re-layouts  16.1 us
    pallas_call x1, Pallas kernels, shards(): pl.pallas_call(state_kernel, out_shape=(jax.ShapeDtypeStruct((rows, width...  14.2 us
    pallas_call x1, Pallas kernels, shards(): pl.pallas_call(near_kernel, grid=(pairs,), out_shape=(jax.ShapeDtypeStruc...  13.7 us
    ppermute x7, starting transfers between devices, crossed(): return lax.ppermute(block, 'seq', [(i, i ^ mask) for i in range(size)])  12.6 us
    pallas_call x1, Pallas kernels, shards(): pl.pallas_call(functools.partial(far_kernel, local_bits + 1), grid=(pairs...  10.8 us
    ppermute x7, waiting for transfers between devices, crossed(): return lax.ppermute(block, 'seq', [(i, i ^ mask) for i in range(size)])  7.5 us
    convert_element_type x3, other arithmetic, shards(): level_states.append((pair.astype(F32) * gate).astype(BF16))  3.3 us
    ppermute x1, starting transfers between devices, shards(): halo = lax.ppermute(rim, 'seq', [(i, i + 1) for i in range(size - 1)])  2.39 us
  transfers between devices with their start and end apart: 8, of which 3 were waited for; matrix products, arithmetic and copies ran while one was open for 8% of the time, Pallas kernels for 15%

profile of v1, /device:TPU:0, one launch (start us, length us, event | category | flops | bytes accessed | tf_op | source)
XLA Modules:
  0.0 91.5 jit_solution(9517845631499243533)
XLA Ops:
  0.0 0.8 slice.38
  0.8 0.1 select_reduce_fusion
  0.9 0.8 slice_multiply_fusion
  1.7 2.4 %collective-permute-start = (bf16[8,1024]{1,0:T(8,128)(2,1)S(1)}, bf16[8,1024]{1,0:T(8,128)(2,1)S(1)}, u32[]{:S(2)}, u32[]{:S(2)}) collective-permute-start(bf16[8,1024]{1,0:T(8,128)(2,1)S(1)} %slice_multiply_fusion), channel_id=1, source_target_pairs={{0,1},{1,2},{2,3},{3,4},{4,5},{5,6},{6,7},{7,8},{8,9},{9,10},{10,1... | collective-permute-start | bytes 49160 | tf_op jit(solution)/shard_map/ppermute | solution.py:246
  4.1 0.8 copy.12.table_ref
  4.9 0.0 collective-permute-done.halo_ref
  4.9 0.0 copy-start.2
  4.9 0.7 copy-done.2
  5.6 0.0 copy-start.5
  5.6 0.7 copy-done.5
  6.3 0.0 copy-start.6
  6.3 0.7 copy-done.6
  7.0 14.2 %conv_key_value_state.1 = (bf16[1024,1024]{1,0:T(8,128)(2,1)S(1)}, bf16[1024,1024]{1,0:T(8,128)(2,1)S(1)}, bf16[1024,1024]{1,0:T(8,128)(2,1)}, f32[1024,128]{1,0...) custom-call(bf16[1024,1024]{1,0:T(8,128)(2,1)} %x_ref.1, ...), custom_call_target="tpu_custom_call" | custom-call | flops 4294967296 | bytes 8388608 | tf_op jit(solution)/shard_map/conv_key_value_state/pallas_call | solution.py:249
  21.2 0.0 copy-start.7
  21.2 1.3 %copy-done.7 = bf16[1024,1024]{1,0:T(8,128)(2,1)} copy-done((bf16[1024,1024]{1,0:T(8,128)(2,1)}, bf16[1024,1024]{1,0:T(8,128)(2,1)S(1)}, u32[]{:S(2)}) %copy-start.7) | copy-done | bytes 2097176
  22.5 1.3 %copy-done.9 = bf16[1024,1024]{1,0:T(8,128)(2,1)} copy-done((bf16[1024,1024]{1,0:T(8,128)(2,1)}, bf16[1024,1024]{1,0:T(8,128)(2,1)S(1)}, u32[]{:S(2)}) %copy-start.9) | copy-done | bytes 2097176
  23.8 0.0 copy-start.12
  23.8 0.9 copy-done.12
  24.7 0.0 copy-start.3
  24.7 2.6 %collective-permute-start.1 = (bf16[2,528,128]{2,1,0:T(8,128)(2,1)S(1)}, bf16[2,528,128]{2,1,0:T(8,128)(2,1)S(1)}, u32[]{:S(2)}, u32[]{:S(2)}) collective-permute-start(bf16[2,528,128]{2,1,0:T(8,128)(2,1)S(1)} %get-tuple-element.20), channel_id=1, source_target_pairs={{0,1},{1,0},{2,3},{3,2},{4,5},{5,4},{6,7},{7,6},{8,9},{9,8},{10,11... | collective-permute-start | bytes 811016 | tf_op jit(solution)/shard_map/ppermute | solution.py:205
  27.4 1.2 %collective-permute-done.1 = bf16[2,528,128]{2,1,0:T(8,128)(2,1)S(1)} collective-permute-done((bf16[2,528,128]{2,1,0:T(8,128)(2,1)S(1)}, bf16[2,528,128]{2,1,0:T(8,128)(2,1)S(1)}, u32[]{:S(2)}, u32[]{:S(2)}) %collective-permute-start.1) | collective-permute-done | bytes 270368 | tf_op jit(solution)/shard_map/ppermute | solution.py:205
  28.6 0.0 copy-start.14
  28.6 0.1 select_convert_fusion
  28.6 0.5 slice.50
  29.7 0.2 add_convert_fusion
  29.9 2.6 %collective-permute-start.2 = (bf16[528,128]{1,0:T(8,128)(2,1)S(1)}, bf16[528,128]{1,0:T(8,128)(2,1)S(1)}, u32[]{:S(2)}, u32[]{:S(2)}) collective-permute-start(bf16[528,128]{1,0:T(8,128)(2,1)S(1)} %fusion), channel_id=1, source_target_pairs={{0,2},{1,3},{2,0},{3,1},{4,6},{5,7},{6,4},{7,5},{8,10},{9,11},{10,... | collective-permute-start | bytes 405512 | tf_op jit(solution)/shard_map/ppermute | solution.py:205
  32.5 0.0 copy-done.3
  32.5 0.3 reduce-window.9
  32.8 0.1 slice.39
  32.9 0.1 slice_reduce_fusion
  33.0 3.4 %collective-permute-done.2 = bf16[528,128]{1,0:T(8,128)(2,1)S(1)} collective-permute-done((bf16[528,128]{1,0:T(8,128)(2,1)S(1)}, bf16[528,128]{1,0:T(8,128)(2,1)S(1)}, u32[]{:S(2)}, u32[]{:S(2)}) %collective-permute-start.2) | collective-permute-done | bytes 135200 | tf_op jit(solution)/shard_map/ppermute | solution.py:205
  36.4 0.5 slice.54
  37.5 0.1 add_convert_fusion.2
  37.6 2.8 %collective-permute-start.4 = (bf16[528,128]{1,0:T(8,128)(2,1)S(1)}, bf16[528,128]{1,0:T(8,128)(2,1)S(1)}, u32[]{:S(2)}, u32[]{:S(2)}) collective-permute-start(bf16[528,128]{1,0:T(8,128)(2,1)S(1)} %add_convert_fusion.2), channel_id=1, source_target_pairs={{0,4},{1,5},{2,6},{3,7},{4,0},{5,1},{6,2},{7,3},{8,12},{9,13},{10,... | collective-permute-start | bytes 405512 | tf_op jit(solution)/shard_map/ppermute | solution.py:205
  40.3 0.1 add_convert_fusion.3
  40.4 0.0 collective-permute-start.3
  40.4 3.0 %collective-permute-done.4 = bf16[528,128]{1,0:T(8,128)(2,1)S(1)} collective-permute-done((bf16[528,128]{1,0:T(8,128)(2,1)S(1)}, bf16[528,128]{1,0:T(8,128)(2,1)S(1)}, u32[]{:S(2)}, u32[]{:S(2)}) %collective-permute-start.4) | collective-permute-done | bytes 135200 | tf_op jit(solution)/shard_map/ppermute | solution.py:205
  43.4 0.0 copy-done.14
  43.4 0.5 slice.56
  44.5 0.7 add_convert_fusion.1
  45.2 4.0 %collective-permute-start.6 = (bf16[528,128]{1,0:T(8,128)(2,1)}, bf16[528,128]{1,0:T(8,128)(2,1)}, u32[]{:S(2)}, u32[]{:S(2)}) collective-permute-start(bf16[528,128]{1,0:T(8,128)(2,1)} %add_convert_fusion.1), channel_id=1, source_target_pairs={{0,12},{1,13},{2,14},{3,15},{4,8},{5,9},{6,10},{7,11},{8,4},{9,5},... | collective-permute-start | bytes 405512 | tf_op jit(solution)/shard_map/ppermute | solution.py:205
  49.2 0.0 collective-permute-start.5
  49.2 0.0 copy-start.4
  49.2 1.6 %copy-done.4 = bf16[1024,1024]{1,0:T(8,128)(2,1)S(1)} copy-done((bf16[1024,1024]{1,0:T(8,128)(2,1)S(1)}, bf16[1024,1024]{1,0:T(8,128)(2,1)}, u32[]{:S(2)}) %copy-start.4) | copy-done | bytes 2097176
  50.8 1.6 %copy-done.8 = bf16[1024,1024]{1,0:T(8,128)(2,1)S(1)} copy-done((bf16[1024,1024]{1,0:T(8,128)(2,1)S(1)}, bf16[1024,1024]{1,0:T(8,128)(2,1)}, u32[]{:S(2)}) %copy-start.8) | copy-done | bytes 2097176
  52.4 1.6 %copy-done.10 = bf16[1024,1024]{1,0:T(8,128)(2,1)S(1)} copy-done((bf16[1024,1024]{1,0:T(8,128)(2,1)S(1)}, bf16[1024,1024]{1,0:T(8,128)(2,1)}, u32[]{:S(2)}) %copy-start.10) | copy-done | bytes 2097176
  54.0 1.6 %copy-done.11 = bf16[1024,1024]{1,0:T(8,128)(2,1)S(1)} copy-done((bf16[1024,1024]{1,0:T(8,128)(2,1)S(1)}, bf16[1024,1024]{1,0:T(8,128)(2,1)}, u32[]{:S(2)}) %copy-start.11) | copy-done | bytes 2097176
  55.6 1.1 %copy-done.13 = bf16[3,1024,128]{2,1,0:T(8,128)(2,1)S(1)} copy-done((bf16[3,1024,128]{2,1,0:T(8,128)(2,1)S(1)}, bf16[3,1024,128]{2,1,0:T(8,128)(2,1)}, u32[]{:S(2)}) %copy-start.13) | copy-done | bytes 786456
  56.7 13.7 %query_near.1 = (bf16[1024,1024]{1,0:T(8,128)(2,1)S(1)}, f32[1024,1024]{1,0:T(8,128)}) custom-call(bf16[1024,1024]{1,0:T(8,128)(2,1)S(1)} %copy-done.8, bf16[1024,1024]{1,0:T(8,128)(2,1)S(1)} %copy-done.4, bf16[1024,1024]{1,0:T(8,128)(2,1)S(1)} %copy-done.10, bf16[1024,1024]{1,0:T(8,128)(2,1)S(1)} %copy-done.11, f32[1024,128]{1,0:T(8,128)S(1)} %get-tuple-element.16.aux_ref, ...), custom_call_target="tpu_custom_call" | custom-call | flops 4294967296 | bytes 8388608 | tf_op jit(solution)/shard_map/query_near/pallas_call | solution.py:313
  70.4 1.2 %slice.53 = bf16[1,1,1]{2,1,0:T(2,128)(2,1)} slice(bf16[2,528,128]{2,1,0:T(8,128)(2,1)} %copy-done.14), slice={[0:1], [527:528], [0:1]} | slice | bytes 4 | tf_op jit(solution)/shard_map/slice | solution.py:217
  72.2 0.5 slice.55
  73.4 0.0 collective-permute-done.6
  73.4 0.6 collective-permute-start.7
  74.0 0.0 collective-permute-done.3
  74.0 1.1 %multiply_convert_fusion.2.refs_1_ = bf16[2,528,128]{2,1,0:T(8,128)(2,1)S(1)} fusion(bf16[1,528,128]{2,1,0:T(8,128)(2,1)S(1)} %bitcast.29, bf16[1,528,128]{2,1,0:T(8,128)(2,1)} %bitcast.7, f32[]{:T(128)S(6)} %mul.71, pred[]{:T(512)S(6)} %eq.28), kind=kLoop, calls=%fused_computation.2 | loop fusion | flops 811008 | bytes 540677 | tf_op jit(solution)/shard_map/convert_element_type | solution.py:304
  75.1 0.5 slice.57
  76.3 0.0 collective-permute-done.5
  76.3 1.1 %multiply_convert_fusion.1.refs_2_ = bf16[2,528,128]{2,1,0:T(8,128)(2,1)S(1)} fusion(bf16[1,528,128]{2,1,0:T(8,128)(2,1)S(1)} %bitcast.28, bf16[1,528,128]{2,1,0:T(8,128)(2,1)} %bitcast.11, f32[]{:T(128)S(6)} %mul.77, pred[]{:T(512)S(6)} %eq.28), kind=kLoop, calls=%fused_computation.1 | loop fusion | flops 811008 | bytes 540677 | tf_op jit(solution)/shard_map/convert_element_type | solution.py:304
  77.3 0.0 collective-permute-done.7
  77.3 1.2 %multiply_convert_fusion.refs_3_ = bf16[2,528,128]{2,1,0:T(8,128)(2,1)S(1)} fusion(bf16[1,528,128]{2,1,0:T(8,128)(2,1)} %bitcast.16, bf16[1,528,128]{2,1,0:T(8,128)(2,1)} %bitcast.15, f32[]{:T(128)S(6)} %mul.83, pred[]{:T(512)S(6)} %eq.28), kind=kLoop, calls=%fused_computation | loop fusion | flops 811008 | bytes 540677 | tf_op jit(solution)/shard_map/convert_element_type | solution.py:304
  78.5 0.0 copy-done.1
  78.5 0.0 copy-start
  78.6 2.2 %copy-done = f32[1024,1024]{1,0:T(8,128)S(1)} copy-done((f32[1024,1024]{1,0:T(8,128)S(1)}, f32[1024,1024]{1,0:T(8,128)}, u32[]{:S(2)}) %copy-start) | copy-done | bytes 4194328
  80.7 10.8 %far_norm.1 = bf16[1024,1024]{1,0:T(8,128)(2,1)} custom-call(bf16[1024,1024]{1,0:T(8,128)(2,1)S(1)} %get-tuple-element.18.q_ref, f32[1024,1024]{1,0:T(8,128)S(1)} %copy-done, f32[1024,128]{1,0:T(8,128)S(1)} %get-tuple-element.16.aux_ref, f32[1,1024]{1,0:T(1,128)S(1)} %bitcast.23, bf16[2,528,128]{2,1,0:T(8,128)(2,1)S(1)} %get-tuple-element.22.refs_0_, ...), custom_call_target="tpu_custom_call" | custom-call | flops 2147483648 | bytes 8388608 | tf_op jit(solution)/shard_map/far_norm/pallas_call | solution.py:339
  (11 shorter events, 0.1 us)
Async XLA Ops:
  1.7 3.2 %collective-permute-start = (bf16[8,1024]{1,0:T(8,128)(2,1)S(1)}, bf16[8,1024]{1,0:T(8,128)(2,1)S(1)}, u32[]{:S(2)}, u32[]{:S(2)}) collective-permute-start(bf16[8,1024]{1,0:T(8,128)(2,1)S(1)} %slice_multiply_fusion), channel_id=1, source_target_pairs={{0,1},{1,2},{2,3},{3,4},{4,5},{5,6},{6,7},{7,8},{8,9},{9,10},{10,1... | collective-permute-start | bytes 49160 | tf_op jit(solution)/shard_map/ppermute | solution.py:246
  4.9 0.7 copy-start.2
  5.6 0.7 copy-start.5
  6.3 0.7 copy-start.6
  21.2 1.3 %copy-start.7 = (bf16[1024,1024]{1,0:T(8,128)(2,1)}, bf16[1024,1024]{1,0:T(8,128)(2,1)S(1)}, u32[]{:S(2)}) copy-start(bf16[1024,1024]{1,0:T(8,128)(2,1)S(1)} %get-tuple-element.13.conv_ref) | copy-start | bytes 6291460
  22.5 1.3 %copy-start.9 = (bf16[1024,1024]{1,0:T(8,128)(2,1)}, bf16[1024,1024]{1,0:T(8,128)(2,1)S(1)}, u32[]{:S(2)}) copy-start(bf16[1024,1024]{1,0:T(8,128)(2,1)S(1)} %get-tuple-element.14.k_ref) | copy-start | bytes 6291460
  23.8 0.9 copy-start.12
  24.7 7.8 %copy-start.3 = (s32[1024]{0:T(1024)S(1)}, s32[1024]{0:T(1024)}, u32[]{:S(2)}) copy-start(s32[1024]{0:T(1024)} %param.10) | copy-start | bytes 12292
  24.7 3.8 %collective-permute-start.1 = (bf16[2,528,128]{2,1,0:T(8,128)(2,1)S(1)}, bf16[2,528,128]{2,1,0:T(8,128)(2,1)S(1)}, u32[]{:S(2)}, u32[]{:S(2)}) collective-permute-start(bf16[2,528,128]{2,1,0:T(8,128)(2,1)S(1)} %get-tuple-element.20), channel_id=1, source_target_pairs={{0,1},{1,0},{2,3},{3,2},{4,5},{5,4},{6,7},{7,6},{8,9},{9,8},{10,11... | collective-permute-start | bytes 811016 | tf_op jit(solution)/shard_map/ppermute | solution.py:205
  28.6 14.8 %copy-start.14 = (bf16[2,528,128]{2,1,0:T(8,128)(2,1)}, bf16[2,528,128]{2,1,0:T(8,128)(2,1)S(1)}, u32[]{:S(2)}) copy-start(bf16[2,528,128]{2,1,0:T(8,128)(2,1)S(1)} %collective-permute-done.1) | copy-start | bytes 811012
  29.9 6.5 %collective-permute-start.2 = (bf16[528,128]{1,0:T(8,128)(2,1)S(1)}, bf16[528,128]{1,0:T(8,128)(2,1)S(1)}, u32[]{:S(2)}, u32[]{:S(2)}) collective-permute-start(bf16[528,128]{1,0:T(8,128)(2,1)S(1)} %fusion), channel_id=1, source_target_pairs={{0,2},{1,3},{2,0},{3,1},{4,6},{5,7},{6,4},{7,5},{8,10},{9,11},{10,... | collective-permute-start | bytes 405512 | tf_op jit(solution)/shard_map/ppermute | solution.py:205
  37.6 5.8 %collective-permute-start.4 = (bf16[528,128]{1,0:T(8,128)(2,1)S(1)}, bf16[528,128]{1,0:T(8,128)(2,1)S(1)}, u32[]{:S(2)}, u32[]{:S(2)}) collective-permute-start(bf16[528,128]{1,0:T(8,128)(2,1)S(1)} %add_convert_fusion.2), channel_id=1, source_target_pairs={{0,4},{1,5},{2,6},{3,7},{4,0},{5,1},{6,2},{7,3},{8,12},{9,13},{10,... | collective-permute-start | bytes 405512 | tf_op jit(solution)/shard_map/ppermute | solution.py:205
  40.4 33.6 %collective-permute-start.3 = (bf16[528,128]{1,0:T(8,128)(2,1)S(1)}, bf16[528,128]{1,0:T(8,128)(2,1)}, u32[]{:S(2)}, u32[]{:S(2)}) collective-permute-start(bf16[528,128]{1,0:T(8,128)(2,1)S(1)} %collective-permute-done.2), channel_id=1, source_target_pairs={{0,1},{1,0},{2,3},{3,2},{4,5},{5,4},{6,7},{7,6},{8,9},{9,8},{10,11... | collective-permute-start | bytes 405512 | tf_op jit(solution)/shard_map/ppermute | solution.py:205
  45.2 28.2 %collective-permute-start.6 = (bf16[528,128]{1,0:T(8,128)(2,1)}, bf16[528,128]{1,0:T(8,128)(2,1)}, u32[]{:S(2)}, u32[]{:S(2)}) collective-permute-start(bf16[528,128]{1,0:T(8,128)(2,1)} %add_convert_fusion.1), channel_id=1, source_target_pairs={{0,12},{1,13},{2,14},{3,15},{4,8},{5,9},{6,10},{7,11},{8,4},{9,5},... | collective-permute-start | bytes 405512 | tf_op jit(solution)/shard_map/ppermute | solution.py:205
  49.2 27.0 %collective-permute-start.5 = (bf16[528,128]{1,0:T(8,128)(2,1)S(1)}, bf16[528,128]{1,0:T(8,128)(2,1)}, u32[]{:S(2)}, u32[]{:S(2)}) collective-permute-start(bf16[528,128]{1,0:T(8,128)(2,1)S(1)} %collective-permute-done.4), channel_id=1, source_target_pairs={{0,1},{1,0},{2,3},{3,2},{4,5},{5,4},{6,7},{7,6},{8,9},{9,8},{10,11... | collective-permute-start | bytes 405512 | tf_op jit(solution)/shard_map/ppermute | solution.py:205
  49.2 1.6 %copy-start.4 = (bf16[1024,1024]{1,0:T(8,128)(2,1)S(1)}, bf16[1024,1024]{1,0:T(8,128)(2,1)}, u32[]{:S(2)}) copy-start(bf16[1024,1024]{1,0:T(8,128)(2,1)} %wq_ref.1) | copy-start | bytes 6291460
  50.8 1.6 %copy-start.8 = (bf16[1024,1024]{1,0:T(8,128)(2,1)S(1)}, bf16[1024,1024]{1,0:T(8,128)(2,1)}, u32[]{:S(2)}) copy-start(bf16[1024,1024]{1,0:T(8,128)(2,1)} %copy-done.7) | copy-start | bytes 6291460
  52.4 1.6 %copy-start.10 = (bf16[1024,1024]{1,0:T(8,128)(2,1)S(1)}, bf16[1024,1024]{1,0:T(8,128)(2,1)}, u32[]{:S(2)}) copy-start(bf16[1024,1024]{1,0:T(8,128)(2,1)} %copy-done.9) | copy-start | bytes 6291460
  54.0 1.6 %copy-start.11 = (bf16[1024,1024]{1,0:T(8,128)(2,1)S(1)}, bf16[1024,1024]{1,0:T(8,128)(2,1)}, u32[]{:S(2)}) copy-start(bf16[1024,1024]{1,0:T(8,128)(2,1)} %get-tuple-element.15.v_ref) | copy-start | bytes 6291460
  55.6 1.1 %copy-start.13 = (bf16[3,1024,128]{2,1,0:T(8,128)(2,1)S(1)}, bf16[3,1024,128]{2,1,0:T(8,128)(2,1)}, u32[]{:S(2)}) copy-start(bf16[3,1024,128]{2,1,0:T(8,128)(2,1)} %copy-done.12) | copy-start | bytes 2359300
  56.7 21.8 %copy-start.1 = (f32[1024]{0:T(1024)S(1)}, f32[1024]{0:T(1024)}, u32[]{:S(2)}) copy-start(f32[1024]{0:T(1024)} %param.17) | copy-start | bytes 12292
  73.4 3.9 %collective-permute-start.7 = (bf16[528,128]{1,0:T(8,128)(2,1)}, bf16[528,128]{1,0:T(8,128)(2,1)}, u32[]{:S(2)}, u32[]{:S(2)}) collective-permute-start(bf16[528,128]{1,0:T(8,128)(2,1)} %collective-permute-done.6), channel_id=1, source_target_pairs={{0,1},{1,0},{2,3},{3,2},{4,5},{5,4},{6,7},{7,6},{8,9},{9,8},{10,11... | collective-permute-start | bytes 405512 | tf_op jit(solution)/shard_map/ppermute | solution.py:205
  78.5 2.2 %copy-start = (f32[1024,1024]{1,0:T(8,128)S(1)}, f32[1024,1024]{1,0:T(8,128)}, u32[]{:S(2)}) copy-start(f32[1024,1024]{1,0:T(8,128)} %get-tuple-element.19.near_ref) | copy-start | bytes 12582916

commit v2 on v0

v2 whole, which is shorter than its diff:
```python
import functools

import jax
import jax.numpy as jnp
from jax import lax
from jax.experimental import pallas as pl
from jax.experimental.pallas import tpu as pltpu
from jax.sharding import PartitionSpec as P

HEADS = 8
HEAD_DIM = 128
CHUNK = 256
RIM = 16
FLAG_ROWS = 16
DOC_COL = 32
PAIR = 2 * HEAD_DIM
highest = lax.Precision.HIGHEST
epsilon = 1e-05
F32 = jnp.float32
BF16 = jnp.bfloat16
VMEM = pl.BlockSpec(memory_space=pltpu.VMEM)
HBM = pl.BlockSpec(memory_space=pltpu.HBM)
NT = ((1,), (1,))
NN = ((1,), (0,))


def dot(a, b, dims=NN, precision=None):
    return lax.dot_general(a, b, (dims, ((), ())), precision=precision, preferred_element_type=F32)


def iota(shape, axis):
    return lax.broadcasted_iota(jnp.int32, shape, axis)


def rim_kernel(x_hbm, ds_hbm, rim_ref, rows_ref, ds_ref, sems):
    rows = x_hbm.shape[0]
    copies = [
        pltpu.make_async_copy(x_hbm.at[rows - RIM : rows, :], rows_ref, sems.at[0]),
        pltpu.make_async_copy(ds_hbm.at[:, rows - 128 : rows], ds_ref, sems.at[1]),
    ]
    for copy in copies:
        copy.start()
    for copy in copies:
        copy.wait()
    starts = jnp.broadcast_to(ds_ref[...].astype(F32), (RIM, 128))
    later = iota((RIM, 128), 1) > iota((RIM, 128), 0) + (128 - RIM)
    cuts = jnp.sum(jnp.where(later, starts, 0.0), axis=1, keepdims=True)
    rim_ref[...] = jnp.where(cuts == 0.0, rows_ref[...].astype(F32), 0.0).astype(BF16)


def project(c, h, conv, wk_ref, wv_ref, k_out, v_out, tail, eye, st_ref):
    cols = slice(h * HEAD_DIM, h * HEAD_DIM + PAIR)
    key = dot(conv, wk_ref[:, cols]).astype(BF16)
    value = dot(conv, wv_ref[:, cols]).astype(BF16)
    k_out[:, cols] = key
    v_out[:, cols] = value
    turned = (dot(eye, key, NT) * tail).astype(BF16)
    for g in range(2):
        lanes = slice(g * HEAD_DIM, (g + 1) * HEAD_DIM)
        st_ref[(h + g) * HEAD_DIM : (h + g + 1) * HEAD_DIM, :] = dot(turned[lanes, :], value[:, lanes])


def identity():
    return (iota((PAIR, PAIR), 0) == iota((PAIR, PAIR), 1)).astype(BF16)


def body_kernel(
    x_hbm, ds_hbm, cw_hbm, wk_hbm, wv_hbm, wq_hbm,
    head_ref, mask_ref, c0_ref, conv_ref, k_ref, v_ref, st_ref, doc_ref, cw_ref, wk_ref, wv_ref, wq_ref,
    x_ref, xs, col_ref, ds_ref, sems,
):
    rows, width = x_ref.shape
    chunks = rows // CHUNK
    taps = cw_hbm.shape[0]
    order = list(range(1, chunks)) + [0]
    small = [
        pltpu.make_async_copy(ds_hbm, ds_ref, sems.at[0]),
        pltpu.make_async_copy(cw_hbm, cw_ref, sems.at[1]),
    ]
    loads = {
        c: pltpu.make_async_copy(
            x_hbm.at[c * CHUNK : (c + 1) * CHUNK, :], x_ref.at[c * CHUNK : (c + 1) * CHUNK, :], sems.at[2 + c]
        )
        for c in range(chunks)
    }
    weights = [
        pltpu.make_async_copy(source, target, sems.at[2 + chunks + n])
        for n, (source, target) in enumerate(((wk_hbm, wk_ref), (wv_hbm, wv_ref), (wq_hbm, wq_ref)))
    ]
    for copy in small:
        copy.start()
    loads[0].start()
    loads[1].start()
    weights[0].start()
    weights[1].start()
    for c in order[1:-1]:
        loads[c].start()
    weights[2].start()
    for copy in small:
        copy.wait()

    starts = jnp.broadcast_to(ds_ref[...].astype(F32), (8, rows))
    lane = iota((8, rows), 1)
    sub = iota((8, rows), 0)
    same = [1.0 - starts]
    for back in range(1, taps - 1):
        same.append(same[-1] * jnp.where(lane < back, 1.0, pltpu.roll(same[0], back, axis=1)))
    packed = jnp.zeros((8, rows), F32)
    for n, m in enumerate(same):
        packed = jnp.where(sub == n, m, packed)
    for c in range(chunks):
        col_ref[c * CHUNK : (c + 1) * CHUNK, 0:8] = packed[:, c * CHUNK : (c + 1) * CHUNK].T
    mask_ref[:, 0:8] = col_ref[0:RIM, 0:8]

    def widen(c):
        xs[c * CHUNK : (c + 1) * CHUNK, :] = x_ref[c * CHUNK : (c + 1) * CHUNK, :].astype(F32)

    def conv_piece(low, count, cols, out, out_low):
        total = xs[low : low + count, cols] * cw_ref[0:1, cols]
        for n in range(1, taps):
            mask = jnp.broadcast_to(col_ref[low : low + count, n - 1 : n], (count, PAIR))
            total = total + (xs[low - n : low - n + count, cols] * cw_ref[n : n + 1, cols]) * mask
        out[out_low : out_low + count, cols] = total.astype(BF16)

    loads[0].wait()
    widen(0)
    head_ref[...] = xs[0:RIM, :]
    loads[1].wait()
    widen(1)
    for h in range(0, HEADS, 2):
        cols = slice(h * HEAD_DIM, h * HEAD_DIM + PAIR)
        conv_piece(CHUNK, CHUNK, cols, conv_ref, 0)
    upper = (iota((CHUNK, CHUNK), 0) <= iota((CHUNK, CHUNK), 1)).astype(BF16)
    base = jnp.zeros((8, 1), F32)
    for c in range(chunks):
        part = dot(starts[:, c * CHUNK : (c + 1) * CHUNK].astype(BF16), upper) + base
        doc_ref[:, c * CHUNK : (c + 1) * CHUNK] = part
        base = part[:, CHUNK - 1 : CHUNK]
    eye = identity()
    weights[0].wait()
    weights[1].wait()
    for n, c in enumerate(order[:-1]):
        low = c * CHUNK
        here = slice(low - CHUNK, low)
        after = order[n + 1]
        if after != 0:
            loads[after].wait()
            widen(after)
        tail = (doc_ref[0:1, low : low + CHUNK] == doc_ref[0:1, low + CHUNK - 1 : low + CHUNK]).astype(F32)
        conv = conv_ref[here, :]
        for h in range(0, HEADS, 2):
            cols = slice(h * HEAD_DIM, h * HEAD_DIM + PAIR)
            if after == 0:
                conv_piece(RIM, CHUNK - RIM, cols, c0_ref, RIM)
            else:
                conv_piece(after * CHUNK, CHUNK, cols, conv_ref, (after - 1) * CHUNK)
            project(c, h, conv, wk_ref, wv_ref, k_ref.at[here, :], v_ref.at[here, :], tail, eye, st_ref.at[c - 1])
    weights[2].wait()


def first_kernel(
    halo_ref, head_ref, mask_ref, c0_ref, st_ref, doc_ref, cw_ref, wk_ref, wv_ref,
    conv_ref, k_ref, v_ref, pay_ref, loc_ref,
    xs, st0,
):
    taps = cw_ref.shape[0]
    chunks = st_ref.shape[0] + 1
    half = HEADS // 2 * HEAD_DIM
    xs[0:RIM, :] = halo_ref[...].astype(F32)
    xs[RIM : 2 * RIM, :] = head_ref[...]
    total = xs[RIM : 2 * RIM, :] * cw_ref[0:1, :]
    for n in range(1, taps):
        total = total + (xs[RIM - n : 2 * RIM - n, :] * cw_ref[n : n + 1, :]) * mask_ref[:, n - 1 : n]
    conv_ref[0:RIM, :] = total.astype(BF16)
    conv_ref[RIM:CHUNK, :] = c0_ref[RIM:CHUNK, :]
    eye = identity()
    tail = (doc_ref[0:1, 0:CHUNK] == doc_ref[0:1, CHUNK - 1 : CHUNK]).astype(F32)
    conv = conv_ref[...]
    for h in range(0, HEADS, 2):
        project(0, h, conv, wk_ref, wv_ref, k_ref, v_ref, tail, eye, st0)

    def end(c):
        return doc_ref[0:1, (c + 1) * CHUNK - 1 : (c + 1) * CHUNK]

    for h in range(HEADS):
        span = slice(h * HEAD_DIM, (h + 1) * HEAD_DIM)
        nodes = [(st0[span, :], 0)] + [(st_ref[c - 1, span, :], c) for c in range(1, chunks)]
        slot = 0
        while len(nodes) > 1:
            merged = []
            for n in range(0, len(nodes), 2):
                (left, left_last), (right, right_last) = nodes[n], nodes[n + 1]
                loc_ref[slot, span, :] = left.astype(BF16)
                slot += 1
                keep = (end(left_last) == end(right_last)).astype(F32)
                merged.append((right + keep * left, right_last))
            nodes = merged
        low = h * HEAD_DIM % half
        pay_ref[h * HEAD_DIM // half, low : low + HEAD_DIM, :] = nodes[0][0].astype(BF16)
    closed = (end(chunks - 1) > 0).astype(F32)
    for n in range(2):
        pay_ref[n, half : half + FLAG_ROWS, :] = jnp.broadcast_to(closed, (FLAG_ROWS, HEAD_DIM)).astype(BF16)


def fill_aux(idx_hbm, table_hbm, doc_ref, aux_ref, weight_ref, flat_ref, idx_ref, table_ref, sems):
    rows = aux_ref.shape[0]
    chunks = rows // CHUNK
    bits = CHUNK.bit_length() - 1
    levels, table_rows = table_hbm.shape
    copies = [
        pltpu.make_async_copy(idx_hbm, idx_ref, sems.at[0]),
        pltpu.make_async_copy(table_hbm, table_ref, sems.at[1]),
    ]
    for copy in copies:
        copy.start()
    flat_ref[DOC_COL : DOC_COL + 8, :] = doc_ref[...]
    for copy in copies:
        copy.wait()
    idx = jnp.broadcast_to(idx_ref[...], (table_rows, rows))
    onehot = (idx == iota((table_rows, rows), 0)).astype(F32)
    flat_ref[0:levels, :] = dot(table_ref[...], onehot, NN, highest)
    t = iota((CHUNK, CHUNK), 0)
    s = iota((CHUNK, CHUNK), 1)
    gap = jnp.bitwise_xor(t, s)
    for c in range(chunks):
        span = slice(c * CHUNK, (c + 1) * CHUNK)
        lam = flat_ref[:, span].T
        aux_ref[span, :] = lam
        w = jnp.broadcast_to(lam[:, 0:1], (CHUNK, CHUNK))
        for level in range(1, bits + 1):
            w = jnp.where(gap >= 1 << (level - 1), lam[:, level : level + 1], w)
        same = (lam[:, DOC_COL : DOC_COL + 1] == doc_ref[0:1, span]) & (t >= s)
        weight_ref[c] = jnp.where(same, w, 0.0)


def near_heads(pairs, convs, keys, values, wq_ref, aux_ref, weight_ref, loc_ref, q_ref, near_ref):
    rows = aux_ref.shape[0]
    chunks = rows // CHUNK
    bits = CHUNK.bit_length() - 1

    def part(refs, c, cols):
        if c == 0:
            return refs[0][:, cols]
        return refs[1][(c - 1) * CHUNK : c * CHUNK, cols]

    for c in range(chunks):
        span = slice(c * CHUNK, (c + 1) * CHUNK)
        lam = aux_ref[span, :]
        doc = lam[:, DOC_COL : DOC_COL + 1]
        gates = []
        slot, count, level = 0, chunks, bits + 1
        while count > 1:
            node = c * count // chunks
            if node % 2 == 1:
                last = node * (chunks // count) * CHUNK - 1
                end = aux_ref[last : last + 1, DOC_COL : DOC_COL + 1]
                gate = jnp.where(doc == end, lam[:, level : level + 1], 0.0)
                gates.append((slot + node // 2, jnp.broadcast_to(gate, (CHUNK, HEAD_DIM))))
            slot += count // 2
            count //= 2
            level += 1
        conv = part(convs, c, slice(None))
        for m, pair in enumerate(pairs):
            cols = slice(pair * PAIR, (pair + 1) * PAIR)
            query = dot(conv, wq_ref[:, cols]).astype(BF16)
            q_ref[span, m * PAIR : (m + 1) * PAIR] = query
            key, value = part(keys, c, cols), part(values, c, cols)
            for g in range(2):
                lanes = slice(g * HEAD_DIM, (g + 1) * HEAD_DIM)
                state = slice(pair * PAIR + g * HEAD_DIM, pair * PAIR + (g + 1) * HEAD_DIM)
                q = query[:, lanes]
                weighted = (dot(q, key[:, lanes], NT) * weight_ref[c]).astype(BF16)
                total = dot(weighted, value[:, lanes])
                if len(gates) == 2:
                    states = jnp.concatenate([loc_ref[n, state, :] for n, _ in gates], axis=1)
                    product = dot(q, states)
                    total = total + gates[0][1] * product[:, :HEAD_DIM] + gates[1][1] * product[:, HEAD_DIM:]
                else:
                    for n, gate in gates:
                        total = total + gate * dot(q, loc_ref[n, state, :])
                near_ref[span, m * PAIR + g * HEAD_DIM : m * PAIR + (g + 1) * HEAD_DIM] = total


def near_first_kernel(
    pairs, idx_hbm, table_hbm, doc_ref, c0, c1, k0, k1, v0, v1, wq_ref, loc_ref,
    q_ref, near_ref, aux_ref, weight_ref,
    flat_ref, idx_ref, table_ref, sems,
):
    fill_aux(idx_hbm, table_hbm, doc_ref, aux_ref, weight_ref, flat_ref, idx_ref, table_ref, sems)
    near_heads(pairs, (c0, c1), (k0, k1), (v0, v1), wq_ref, aux_ref, weight_ref, loc_ref, q_ref, near_ref)


def near_next_kernel(pairs, c0, c1, k0, k1, v0, v1, wq_ref, loc_ref, aux_ref, weight_ref, q_ref, near_ref):
    near_heads(pairs, (c0, c1), (k0, k1), (v0, v1), wq_ref, aux_ref, weight_ref, loc_ref, q_ref, near_ref)


def joined(own, other, is_right):
    own, other = own.astype(F32), other.astype(F32)
    right = jnp.where(is_right, own, other)
    left = jnp.where(is_right, other, own)
    keep = 1.0 - right[right.shape[0] - 1 :, :]
    return right + keep * left


def join_first_kernel(own_ref, other_ref, out_ref):
    core = lax.axis_index("seq") % 2
    own = jnp.where(core == 1, own_ref[1], own_ref[0])
    other = jnp.where(core == 1, other_ref[1], other_ref[0])
    out_ref[...] = joined(own, other, core == 1).astype(BF16)


def join_kernel(bit, own_ref, other_ref, out_ref):
    out_ref[...] = joined(own_ref[...], other_ref[...], (lax.axis_index("seq") >> bit) % 2 == 1).astype(BF16)


def far_kernel(first_level, steps, q_a, near_a, q_b, near_b, aux_ref, gain_hbm, *refs):
    whole, parts = refs[0], refs[1 : 2 * steps - 1]
    out_hbm, out_ref, gain_ref, sems = refs[2 * steps - 1 :]
    rows, width = out_ref.shape
    half = width // 2
    chunks = rows // CHUNK
    copy = pltpu.make_async_copy(gain_hbm, gain_ref, sems.at[chunks])
    copy.start()
    me = lax.axis_index("seq")
    core = me % 2
    before = jnp.ones((1, HEAD_DIM), F32)
    marks = []
    for n in range(steps):
        bit = jnp.broadcast_to(((me >> n) % 2).astype(F32), (1, HEAD_DIM))
        flag = (whole[0] if n == 0 else parts[2 * n - 2][...])[half : half + 1, :].astype(F32)
        marks.append(bit * before)
        before = before * (1.0 - bit * flag)
    copy.wait()
    stores = []
    for c in range(chunks):
        span = slice(c * CHUNK, (c + 1) * CHUNK)
        lam = aux_ref[span, :]
        gate = (lam[:, DOC_COL : DOC_COL + 1] == 0.0).astype(F32)
        scales = [
            jnp.broadcast_to(lam[:, first_level + n : first_level + n + 1] * gate, (CHUNK, HEAD_DIM)) * marks[n]
            for n in range(steps)
        ]
        for h in range(HEADS):
            q_ref, near_ref = ((q_a, near_a), (q_b, near_b))[h * HEAD_DIM // half]
            low = h * HEAD_DIM % half
            lanes = slice(low, low + HEAD_DIM)
            states = [whole[h * HEAD_DIM // half, lanes, :]]
            for n in range(1, steps):
                mine, mate = parts[2 * n - 2], parts[2 * n - 1]
                low_half = h * HEAD_DIM < half
                states.append(jnp.where((core == 0) == low_half, mine[lanes, :], mate[lanes, :]))
            q = q_ref[span, lanes]
            total = near_ref[span, lanes]
            for n in range(0, steps, 2):
                group = states[n : n + 2]
                product = dot(q, jnp.concatenate(group, axis=1) if len(group) > 1 else group[0])
                for m in range(len(group)):
                    total = total + scales[n + m] * product[:, m * HEAD_DIM : (m + 1) * HEAD_DIM]
            mean = jnp.mean(total * total, axis=-1, keepdims=True)
            cols = slice(h * HEAD_DIM, (h + 1) * HEAD_DIM)
            out_ref[span, cols] = (total * lax.rsqrt(mean + epsilon) * gain_ref[0:1, cols]).astype(BF16)
        store = pltpu.make_async_copy(out_ref.at[span, :], out_hbm.at[span, :], sems.at[c])
        store.start()
        stores.append(store)
    for store in stores:
        store.wait()


def crossed(block, mask):
    size = lax.axis_size("seq")
    return lax.ppermute(block, "seq", [(i, i ^ mask) for i in range(size)])


def pinned(array):
    return pltpu.with_memory_space_constraint(array, pltpu.HBM)


def cost(flops, moved):
    return pl.CostEstimate(flops=flops, bytes_accessed=moved, transcendentals=0)


def params(mib):
    return pltpu.CompilerParams(vmem_limit_bytes=mib << 20)


def shards(
    tokens,
    doc_start,
    level_index,
    level_table,
    conv_weight,
    query_weight,
    key_weight,
    value_weight,
    norm_gain,
):
    rows, width = tokens.shape
    taps = conv_weight.shape[0]
    table_rows, levels = level_table.shape
    chunks = rows // CHUNK
    rest = rows - CHUNK
    local_bits = rows.bit_length() - 1
    half = width // 2
    size = lax.axis_size("seq")
    steps = size.bit_length() - 1
    unit = 2 * rows * width * width
    starts = pinned(doc_start.reshape(1, rows))
    tokens = pinned(tokens)
    shape = jax.ShapeDtypeStruct

    rim = pl.pallas_call(
        rim_kernel,
        out_shape=shape((RIM, width), BF16),
        in_specs=[HBM, HBM],
        out_specs=VMEM,
        scratch_shapes=[
            pltpu.VMEM((RIM, width), BF16),
            pltpu.VMEM((1, 128), jnp.int32),
            pltpu.SemaphoreType.DMA((2,)),
        ],
        compiler_params=params(2),
        name="rim",
    )(tokens, starts)
    halo = lax.ppermute(rim, "seq", [(i, i + 1) for i in range(size - 1)])

    head, mask, c0_part, conv_rest, key_rest, value_rest, states, docs, taps_w, wk, wv, wq = pl.pallas_call(
        body_kernel,
        out_shape=(
            shape((RIM, width), F32),
            shape((RIM, 128), F32),
            shape((CHUNK, width), BF16),
            shape((rest, width), BF16),
            shape((rest, width), BF16),
            shape((rest, width), BF16),
            shape((chunks - 1, HEADS * HEAD_DIM, HEAD_DIM), F32),
            shape((8, rows), F32),
            shape((taps, width), F32),
            shape((width, width), BF16),
            shape((width, width), BF16),
            shape((width, width), BF16),
        ),
        in_specs=[HBM] * 6,
        out_specs=(VMEM,) * 12,
        scratch_shapes=[
            pltpu.VMEM((rows, width), BF16),
            pltpu.VMEM((rows, width), F32),
            pltpu.VMEM((rows, 128), F32),
            pltpu.VMEM((1, rows), jnp.int32),
            pltpu.SemaphoreType.DMA((5 + chunks,)),
        ],
        compiler_params=params(24),
        cost_estimate=cost(2 * unit, 8 * width * width),
        name="body",
    )(tokens, starts, pinned(conv_weight), pinned(key_weight), pinned(value_weight), pinned(query_weight))

    conv0, key0, value0, payload, local_states = pl.pallas_call(
        first_kernel,
        out_shape=(
            shape((CHUNK, width), BF16),
            shape((CHUNK, width), BF16),
            shape((CHUNK, width), BF16),
            shape((2, half + FLAG_ROWS, HEAD_DIM), BF16),
            shape((chunks - 1, HEADS * HEAD_DIM, HEAD_DIM), BF16),
        ),
        in_specs=[VMEM] * 9,
        out_specs=(VMEM,) * 5,
        scratch_shapes=[pltpu.VMEM((2 * RIM, width), F32), pltpu.VMEM((HEADS * HEAD_DIM, HEAD_DIM), F32)],
        compiler_params=params(12),
        cost_estimate=cost(unit, width * width),
        name="first",
    )(halo, head, mask, c0_part, states, docs, taps_w, wk, wv)

    def join(kernel, own, other, name):
        return pl.pallas_call(
            kernel,
            out_shape=shape((half + FLAG_ROWS, HEAD_DIM), BF16),
            in_specs=[VMEM, VMEM],
            out_specs=VMEM,
            compiler_params=params(4),
            cost_estimate=cost(1000, 1000),
            name=name,
        )(own, other)

    other = crossed(payload, 1)
    agg = join(join_first_kernel, payload, other, "join_first")
    far_states = [other]
    for bit in range(1, steps):
        last = bit == steps - 1
        across = 1 << bit
        if last and bit >= 2:
            across |= 1 << (bit - 1)
        other = crossed(agg, across)
        far_states += [other, crossed(other, 1)]
        if not last:
            agg = join(functools.partial(join_kernel, bit), agg, other, "join")

    pairs = HEADS // 2
    shared = (conv0, conv_rest, key0, key_rest, value0, value_rest, wq, local_states)
    query_a, near_a, aux, weight = pl.pallas_call(
        functools.partial(near_first_kernel, tuple(range(pairs // 2))),
        out_shape=(
            shape((rows, half), BF16),
            shape((rows, half), F32),
            shape((rows, 128), F32),
            shape((chunks, CHUNK, CHUNK), F32),
        ),
        in_specs=[HBM, HBM] + [VMEM] * 9,
        out_specs=(VMEM,) * 4,
        scratch_shapes=[
            pltpu.VMEM((128, rows), F32),
            pltpu.VMEM((1, rows), jnp.int32),
            pltpu.VMEM((levels, table_rows), F32),
            pltpu.SemaphoreType.DMA((2,)),
        ],
        compiler_params=params(16),
        cost_estimate=cost(unit, width * width),
        name="near_first",
    )(level_index.reshape(1, rows), level_table.T, docs, *shared)
    query_b, near_b = pl.pallas_call(
        functools.partial(near_next_kernel, tuple(range(pairs // 2, pairs))),
        out_shape=(shape((rows, half), BF16), shape((rows, half), F32)),
        in_specs=[VMEM] * 10,
        out_specs=(VMEM,) * 2,
        compiler_params=params(16),
        cost_estimate=cost(unit, width * width),
        name="near_next",
    )(*shared, aux, weight)

    return pl.pallas_call(
        functools.partial(far_kernel, local_bits + 1, steps),
        out_shape=shape((rows, width), BF16),
        in_specs=[VMEM] * 5 + [HBM] + [VMEM] * (2 * steps - 1),
        out_specs=HBM,
        scratch_shapes=[
            pltpu.VMEM((rows, width), BF16),
            pltpu.VMEM((1, width), F32),
            pltpu.SemaphoreType.DMA((chunks + 1,)),
        ],
        compiler_params=params(26),
        cost_estimate=cost(unit, width * width),
        name="far_norm",
    )(query_a, near_a, query_b, near_b, aux, norm_gain.reshape(1, width), *far_states)


def solution(mesh):
    split = P(("groups", "seq"))
    in_specs = (P(("groups", "seq"), None), split, split, P(), P(), P(), P(), P(), P())
    return jax.shard_map(
        shards, mesh=mesh, in_specs=in_specs, out_specs=P(("groups", "seq"), None), check_vma=False
    )
```

time: 120 us -> 54.3 us (0.45)
  the two profiles are of different devices: /device:TPU:24 before, /device:TPU:0 now
where the time goes in v2:
time: 54.3 us; the launch traced here: 54.1 us
  Pallas kernels  32.2 us (59%)
  starting transfers between devices  12.6 us (23%)
  waiting for transfers between devices  8.96 us (17%)
    pallas_call x1, Pallas kernels, shards(): pl.pallas_call(functools.partial(far_kernel, local_bits + 1, steps), out_...  10.5 us
    ppermute x7, starting transfers between devices, crossed(): return lax.ppermute(block, 'seq', [(i, i ^ mask) for i in range(size)])  10.2 us
    pallas_call x1, Pallas kernels, shards(): pl.pallas_call(body_kernel, out_shape=(shape((RIM, width), F32), shape((R...  10.2 us
    ppermute x7, waiting for transfers between devices, crossed(): return lax.ppermute(block, 'seq', [(i, i ^ mask) for i in range(size)])  8.96 us
    pallas_call x1, Pallas kernels, shards(): pl.pallas_call(functools.partial(near_first_kernel, tuple(range(pairs //...  4.34 us
    pallas_call x1, Pallas kernels, shards(): pl.pallas_call(functools.partial(near_next_kernel, tuple(range(pairs // 2...  3.9 us
    ppermute x1, starting transfers between devices, shards(): halo = lax.ppermute(rim, 'seq', [(i, i + 1) for i in range(size - 1)])  2.4 us
    pallas_call x1, Pallas kernels, shards(): pl.pallas_call(first_kernel, out_shape=(shape((CHUNK, width), BF16), shap...  2.24 us
  transfers between devices with their start and end apart: 8, of which 3 were waited for; matrix products, arithmetic and copies ran while one was open for 0% of the time, Pallas kernels for 34%

profile of v2, /device:TPU:0, one launch (start us, length us, event | category | flops | bytes accessed | tf_op | source)
XLA Modules:
  0.0 54.1 jit_solution(7253737818303959111)
XLA Ops:
  0.0 0.9 %rim.1 = bf16[16,1024]{1,0:T(8,128)(2,1)S(1)} custom-call(bf16[1024,1024]{1,0:T(8,128)(2,1)} %x_hbm.3, s32[1,1024]{1,0:T(1,128)} %bitcast.7), custom_call_target="tpu_custom_call" | custom-call | tf_op jit(solution)/shard_map/rim/pallas_call | solution.py:411
  0.9 2.4 %collective-permute-start = (bf16[16,1024]{1,0:T(8,128)(2,1)S(1)}, bf16[16,1024]{1,0:T(8,128)(2,1)S(1)}, u32[]{:S(2)}, u32[]{:S(2)}) collective-permute-start(bf16[16,1024]{1,0:T(8,128)(2,1)S(1)} %rim.1), channel_id=1, source_target_pairs={{0,1},{1,2},{2,3},{3,4},{4,5},{5,6},{6,7},{7,8},{8,9},{9,10},{10,1... | collective-permute-start | bytes 98312 | tf_op jit(solution)/shard_map/ppermute | solution.py:424
  3.3 10.2 %body.1 = (f32[16,1024]{1,0:T(8,128)S(1)}, f32[16,128]{1,0:T(8,128)S(1)}, bf16[256,1024]{1,0:T(8,128)(2,1)S(1)}, bf16[768,1024]{1,0:T(8,128)(2,1)S(1)}, bf16[768...) custom-call(bf16[1024,1024]{1,0:T(8,128)(2,1)} %x_hbm.3, ...), custom_call_target="tpu_custom_call" | custom-call | flops 4294967296 | bytes 8388608 | tf_op jit(solution)/shard_map/body/pallas_call | solution.py:426
  13.4 0.0 collective-permute-done.halo_ref
  13.5 0.0 copy-start
  13.5 0.0 copy-start.1
  13.5 2.2 %first.1 = (bf16[256,1024]{1,0:T(8,128)(2,1)S(1)}, bf16[256,1024]{1,0:T(8,128)(2,1)S(1)}, bf16[256,1024]{1,0:T(8,128)(2,1)S(1)}, bf16[2,528,128]{2,1,0:T(8,128)(2,1)S(1)}, bf16[3,1024,128]{2,1,0:T(8,128)(2,1)S(1)}) custom-call(bf16[16,1024]{1,0:T(8,128)(2,1)S(1)} %collective-permute-done.halo_ref, f32[16,1024]{1,0:T(8,128)S(1)} %get-tuple-element.29.head_ref, ...), custom_call_target="tpu_custom_call" | custom-call | flops 2147483648 | bytes 1048576 | tf_op jit(solution)/shard_map/first/pallas_call | solution.py:456
  15.7 2.7 %collective-permute-start.1 = (bf16[2,528,128]{2,1,0:T(8,128)(2,1)S(1)}, bf16[2,528,128]{2,1,0:T(8,128)(2,1)S(1)}, u32[]{:S(2)}, u32[]{:S(2)}) collective-permute-start(bf16[2,528,128]{2,1,0:T(8,128)(2,1)S(1)} %get-tuple-element.50.own_ref), channel_id=1, source_target_pairs={{0,1},{1,0},{2,3},{3,2},{4,5},{5,4},{6,7},{7,6},{8,9},{9,8},{10,11... | collective-permute-start | bytes 811016 | tf_op jit(solution)/shard_map/ppermute | solution.py:371
  18.4 1.2 %collective-permute-done.1.other_ref.refs_0_ = bf16[2,528,128]{2,1,0:T(8,128)(2,1)S(1)} collective-permute-done((bf16[2,528,128]{2,1,0:T(8,128)(2,1)S(1)}, bf16[2,528,128]{2,1,0:T(8,128)(2,1)S(1)}, u32[]{:S(2)}, u32[]{:S(2)}) %collective-permute-start.1) | collective-permute-done | bytes 270368 | tf_op jit(solution)/shard_map/ppermute | solution.py:371
  19.6 0.1 join_first.1.own_ref
  19.7 1.6 %collective-permute-start.2 = (bf16[528,128]{1,0:T(8,128)(2,1)S(1)}, bf16[528,128]{1,0:T(8,128)(2,1)S(1)}, u32[]{:S(2)}, u32[]{:S(2)}) collective-permute-start(bf16[528,128]{1,0:T(8,128)(2,1)S(1)} %join_first.1.own_ref), channel_id=1, source_target_pairs={{0,2},{1,3},{2,0},{3,1},{4,6},{5,7},{6,4},{7,5},{8,10},{9,11},{10,... | collective-permute-start | bytes 405512 | tf_op jit(solution)/shard_map/ppermute | solution.py:371
  21.2 4.3 %collective-permute-done.2.other_ref.refs_1_ = bf16[528,128]{1,0:T(8,128)(2,1)S(1)} collective-permute-done((bf16[528,128]{1,0:T(8,128)(2,1)S(1)}, bf16[528,128]{1,0:T(8,128)(2,1)S(1)}, u32[]{:S(2)}, u32[]{:S(2)}) %collective-permute-start.2) | collective-permute-done | bytes 135200 | tf_op jit(solution)/shard_map/ppermute | solution.py:371
  25.6 0.1 join.2.own_ref
  25.7 1.6 %collective-permute-start.4 = (bf16[528,128]{1,0:T(8,128)(2,1)S(1)}, bf16[528,128]{1,0:T(8,128)(2,1)S(1)}, u32[]{:S(2)}, u32[]{:S(2)}) collective-permute-start(bf16[528,128]{1,0:T(8,128)(2,1)S(1)} %join.2.own_ref), channel_id=1, source_target_pairs={{0,4},{1,5},{2,6},{3,7},{4,0},{5,1},{6,2},{7,3},{8,12},{9,13},{10,... | collective-permute-start | bytes 405512 | tf_op jit(solution)/shard_map/ppermute | solution.py:371
  27.3 3.4 %collective-permute-done.4.other_ref.refs_3_ = bf16[528,128]{1,0:T(8,128)(2,1)S(1)} collective-permute-done((bf16[528,128]{1,0:T(8,128)(2,1)S(1)}, bf16[528,128]{1,0:T(8,128)(2,1)S(1)}, u32[]{:S(2)}, u32[]{:S(2)}) %collective-permute-start.4) | collective-permute-done | bytes 135200 | tf_op jit(solution)/shard_map/ppermute | solution.py:371
  30.8 0.1 join.3
  30.8 3.7 %collective-permute-start.6 = (bf16[528,128]{1,0:T(8,128)(2,1)S(1)}, bf16[528,128]{1,0:T(8,128)(2,1)S(1)}, u32[]{:S(2)}, u32[]{:S(2)}) collective-permute-start(bf16[528,128]{1,0:T(8,128)(2,1)S(1)} %join.3), channel_id=1, source_target_pairs={{0,12},{1,13},{2,14},{3,15},{4,8},{5,9},{6,10},{7,11},{8,4},{9,5},... | collective-permute-start | bytes 405512 | tf_op jit(solution)/shard_map/ppermute | solution.py:371
  34.5 0.0 copy-done
  34.5 0.0 copy-done.1
  34.5 4.3 %near_first.1 = (bf16[1024,512]{1,0:T(8,128)(2,1)S(1)}, f32[1024,512]{1,0:T(8,128)S(1)}, f32[1024,128]{1,0:T(8,128)S(1)}, f32[4,256,256]{2,1,0:T(8,128)S(1)}) custom-call(s32[1,1024]{1,0:T(1,128)S(1)} %bitcast.5, f32[18,64]{1,0:T(8,128)S(1)} %bitcast.4, f32[8,1024]{1,0:T(8,128)S(1)} %get-tuple-element.28.doc_ref, ...), custom_call_target="tpu_custom_call" | custom-call | flops 2147483648 | bytes 1048576 | tf_op jit(solution)/shard_map/near_first/pallas_call | solution.py:499
  38.9 0.1 collective-permute-start.3
  39.0 0.5 collective-permute-start.5
  39.5 0.0 collective-permute-done.6.refs_5_
  39.5 0.1 collective-permute-start.7
  39.5 0.0 copy-start.2
  39.5 3.9 %near_next.1 = (bf16[1024,512]{1,0:T(8,128)(2,1)S(1)}, f32[1024,512]{1,0:T(8,128)S(1)}) custom-call(bf16[256,1024]{1,0:T(8,128)(2,1)S(1)} %get-tuple-element.36.c0, bf16[768,1024]{1,0:T(8,128)(2,1)S(1)} %get-tuple-element.37.c1, bf16[256,1024]{1,0:T(8,128)(2,1)S(1)} %get-tuple-element.38.k0, bf16[768,1024]{1,0:T(8,128)(2,1)S(1)} %get-tuple-element.39.k1, ...), custom_call_target="tpu_custom_call" | custom-call | flops 2147483648 | bytes 1048576 | tf_op jit(solution)/shard_map/near_next/pallas_call | solution.py:519
  43.4 0.0 collective-permute-done.3.refs_2_
  43.4 0.0 collective-permute-done.5.refs_4_
  43.5 0.0 collective-permute-done.7.refs_6_
  43.5 0.0 copy-done.2
  43.5 10.5 %far_norm.1 = bf16[1024,1024]{1,0:T(8,128)(2,1)} custom-call(bf16[1024,512]{1,0:T(8,128)(2,1)S(1)} %get-tuple-element.44.q_a, f32[1024,512]{1,0:T(8,128)S(1)} %get-tuple-element.45.near_a, bf16[1024,512]{1,0:T(8,128)(2,1)S(1)} %get-tuple-element.48.q_b, f32[1024,512]{1,0:T(8,128)S(1)} %get-tuple-element.49.near_b, ...), custom_call_target="tpu_custom_call" | custom-call | flops 2147483648 | bytes 1048576 | tf_op jit(solution)/shard_map/far_norm/pallas_call | solution.py:529
Async XLA Ops:
  0.9 12.6 %collective-permute-start = (bf16[16,1024]{1,0:T(8,128)(2,1)S(1)}, bf16[16,1024]{1,0:T(8,128)(2,1)S(1)}, u32[]{:S(2)}, u32[]{:S(2)}) collective-permute-start(bf16[16,1024]{1,0:T(8,128)(2,1)S(1)} %rim.1), channel_id=1, source_target_pairs={{0,1},{1,2},{2,3},{3,4},{4,5},{5,6},{6,7},{7,8},{8,9},{9,10},{10,1... | collective-permute-start | bytes 98312 | tf_op jit(solution)/shard_map/ppermute | solution.py:424
  13.5 21.1 %copy-start = (f32[64,18]{0,1:T(8,128)S(1)}, f32[64,18]{0,1:T(8,128)}, u32[]{:S(2)}) copy-start(f32[64,18]{0,1:T(8,128)} %param.12) | copy-start | bytes 13828
  13.5 21.1 %copy-start.1 = (s32[1024]{0:T(1024)S(1)}, s32[1024]{0:T(1024)}, u32[]{:S(2)}) copy-start(s32[1024]{0:T(1024)} %param.11) | copy-start | bytes 12292
  15.7 3.8 %collective-permute-start.1 = (bf16[2,528,128]{2,1,0:T(8,128)(2,1)S(1)}, bf16[2,528,128]{2,1,0:T(8,128)(2,1)S(1)}, u32[]{:S(2)}, u32[]{:S(2)}) collective-permute-start(bf16[2,528,128]{2,1,0:T(8,128)(2,1)S(1)} %get-tuple-element.50.own_ref), channel_id=1, source_target_pairs={{0,1},{1,0},{2,3},{3,2},{4,5},{5,4},{6,7},{7,6},{8,9},{9,8},{10,11... | collective-permute-start | bytes 811016 | tf_op jit(solution)/shard_map/ppermute | solution.py:371
  19.7 5.9 %collective-permute-start.2 = (bf16[528,128]{1,0:T(8,128)(2,1)S(1)}, bf16[528,128]{1,0:T(8,128)(2,1)S(1)}, u32[]{:S(2)}, u32[]{:S(2)}) collective-permute-start(bf16[528,128]{1,0:T(8,128)(2,1)S(1)} %join_first.1.own_ref), channel_id=1, source_target_pairs={{0,2},{1,3},{2,0},{3,1},{4,6},{5,7},{6,4},{7,5},{8,10},{9,11},{10,... | collective-permute-start | bytes 405512 | tf_op jit(solution)/shard_map/ppermute | solution.py:371
  25.7 5.1 %collective-permute-start.4 = (bf16[528,128]{1,0:T(8,128)(2,1)S(1)}, bf16[528,128]{1,0:T(8,128)(2,1)S(1)}, u32[]{:S(2)}, u32[]{:S(2)}) collective-permute-start(bf16[528,128]{1,0:T(8,128)(2,1)S(1)} %join.2.own_ref), channel_id=1, source_target_pairs={{0,4},{1,5},{2,6},{3,7},{4,0},{5,1},{6,2},{7,3},{8,12},{9,13},{10,... | collective-permute-start | bytes 405512 | tf_op jit(solution)/shard_map/ppermute | solution.py:371
  30.8 8.6 %collective-permute-start.6 = (bf16[528,128]{1,0:T(8,128)(2,1)S(1)}, bf16[528,128]{1,0:T(8,128)(2,1)S(1)}, u32[]{:S(2)}, u32[]{:S(2)}) collective-permute-start(bf16[528,128]{1,0:T(8,128)(2,1)S(1)} %join.3), channel_id=1, source_target_pairs={{0,12},{1,13},{2,14},{3,15},{4,8},{5,9},{6,10},{7,11},{8,4},{9,5},... | collective-permute-start | bytes 405512 | tf_op jit(solution)/shard_map/ppermute | solution.py:371
  38.9 4.6 %collective-permute-start.3 = (bf16[528,128]{1,0:T(8,128)(2,1)S(1)}, bf16[528,128]{1,0:T(8,128)(2,1)S(1)}, u32[]{:S(2)}, u32[]{:S(2)}) collective-permute-start(bf16[528,128]{1,0:T(8,128)(2,1)S(1)} %collective-permute-done.2.other_ref.refs_1_), channel_id=1, source_target_pairs={{0,1},{1,0},{2,3},{3,2},{4,5},{5,4},{6,7},{7,6},{8,9},{9,8},{10,11... | collective-permute-start | bytes 405512 | tf_op jit(solution)/shard_map/ppermute | solution.py:371
  39.0 4.5 %collective-permute-start.5 = (bf16[528,128]{1,0:T(8,128)(2,1)S(1)}, bf16[528,128]{1,0:T(8,128)(2,1)S(1)}, u32[]{:S(2)}, u32[]{:S(2)}) collective-permute-start(bf16[528,128]{1,0:T(8,128)(2,1)S(1)} %collective-permute-done.4.other_ref.refs_3_), channel_id=1, source_target_pairs={{0,1},{1,0},{2,3},{3,2},{4,5},{5,4},{6,7},{7,6},{8,9},{9,8},{10,11... | collective-permute-start | bytes 405512 | tf_op jit(solution)/shard_map/ppermute | solution.py:371
  39.5 4.0 %collective-permute-start.7 = (bf16[528,128]{1,0:T(8,128)(2,1)S(1)}, bf16[528,128]{1,0:T(8,128)(2,1)S(1)}, u32[]{:S(2)}, u32[]{:S(2)}) collective-permute-start(bf16[528,128]{1,0:T(8,128)(2,1)S(1)} %collective-permute-done.6.refs_5_), channel_id=1, source_target_pairs={{0,1},{1,0},{2,3},{3,2},{4,5},{5,4},{6,7},{7,6},{8,9},{9,8},{10,11... | collective-permute-start | bytes 405512 | tf_op jit(solution)/shard_map/ppermute | solution.py:371
  39.5 3.9 %copy-start.2 = (f32[1024]{0:T(1024)S(1)}, f32[1024]{0:T(1024)}, u32[]{:S(2)}) copy-start(f32[1024]{0:T(1024)} %param.17) | copy-start | bytes 12292
